TPU v7x, 512 devices: a whole 4x4x16 slice. The times are simulated.
512 devices in a mesh: wide: 64 (over z, y), narrow: 8 (over x, core).
Axes of the slice: x: 4, y: 4, z: 16, core: 2. Of those that a mesh axis runs over, the one named last changes fastest.
Arguments:
- self_block: bfloat16 [2048, 256, 256], P(('wide', 'narrow')), may hold values from -6 to 6
- cross_block: bfloat16 [2048, 256, 512], P(('wide', 'narrow')), may hold values from -0.25 to 0.25
- redundant_inverse: bfloat16 [2048, 512, 512], P(('wide', 'narrow')), may hold values from -6 to 6
- link_block: bfloat16 [2048, 256, 256], P(('wide', 'narrow')), may hold values from -0.3125 to 0.3125
- projection: bfloat16 [2048, 64, 256], P(('wide', 'narrow')), may hold values from -0.375 to 0.375
- parent_far: bfloat16 [512, 256, 256], P(('wide', 'narrow')), may hold values from -6 to 6
- point_count: int32 [2048], P(('wide', 'narrow')), may hold values from 64 to 256, as said below
- box_count: int32 [512], P(('wide', 'narrow')), may hold values from 1 to 4, as said below
Outputs:
- skeleton_blocks: bfloat16 [2048, 256, 256], P(('wide', 'narrow'))
- parent_blocks: bfloat16 [512, 256, 256], P(('wide', 'narrow'))
Inputs may be any that keep to these rules, and one draw needn't show every extreme that they name: `point_count`: some box has exactly 256 live points and some exactly 64; the live points of a box are its first ones. `box_count`: A device's live boxes fill its first slots; some device has all 4 slots live.
All inputs are finite; a program needn't handle non-finite values.
Results may differ from a plain program's by a relative error of at most 0.015.
Values may be sent and summed in bfloat16 or wider, within the bound.
A program may use at most 64 MiB of HBM per device.

v0:
```python
import jax
import jax.numpy as jnp
from jax import lax
from jax.sharding import PartitionSpec as P

SWEEPS = 4


def shifted(shard, axis, by):
    length = lax.axis_size(axis)
    return lax.ppermute(shard, axis, [(i, (i + by) % length) for i in range(length)])


def from_partner(block, axis, bit):
    count = lax.axis_size(axis)
    route = []
    for low in range(count):
        high = low | 1 << bit
        if high != low and high < count:
            route += [(low, high), (high, low)]
    return lax.ppermute(block, axis, route)


def lower_term(lower_state, lower_link):
    lowpart = jnp.einsum(
        "sij,sjk->sik", lower_state, lower_link, preferred_element_type=jnp.float32
    ).astype(jnp.bfloat16)
    return jnp.einsum(
        "sji,sjk->sik", lower_link, lowpart, preferred_element_type=jnp.float32
    ).astype(jnp.bfloat16)


def local(
    self_block,
    cross_block,
    redundant_inverse,
    link_block,
    projection,
    parent_far,
    point_count,
    box_count,
):
    slot_count = self_block.shape[0]
    points = self_block.shape[1]
    kept_points = projection.shape[1]
    positions = jnp.arange(points, dtype=jnp.int32)
    point_mask = (positions[None, :] < point_count[:, None]).astype(jnp.float32)
    live_flag = (jnp.arange(slot_count, dtype=jnp.int32) < box_count[0]).astype(jnp.float32)
    outer_mask = point_mask[:, :, None] * point_mask[:, None, :]
    carried = jnp.einsum(
        "skr,srq->skq", cross_block, redundant_inverse, preferred_element_type=jnp.float32
    ).astype(jnp.bfloat16)
    update = jnp.einsum("skr,sjr->skj", carried, cross_block, preferred_element_type=jnp.float32)
    local_all = (
        live_flag[:, None, None] * outer_mask * (self_block.astype(jnp.float32) - update)
    ).astype(jnp.bfloat16)
    identity = jnp.eye(points, dtype=jnp.float32)
    diag_fill = identity[None, :, :] * (1.0 - live_flag[:, None] * point_mask)[:, None, :]
    live_mask = live_flag[:, None, None] * outer_mask
    local_wide = local_all.astype(jnp.float32)
    state = local_all
    for sweep in range(SWEEPS):
        lower_state, lower_link = shifted((state, link_block), "wide", 1)
        from_lower = lower_term(lower_state, lower_link)
        upper_state = shifted(state, "wide", -1)
        uppart = jnp.einsum(
            "sij,skj->sik", upper_state, link_block, preferred_element_type=jnp.float32
        ).astype(jnp.bfloat16)
        from_upper = jnp.einsum(
            "sij,sjk->sik", link_block, uppart, preferred_element_type=jnp.float32
        )
        total = live_mask * (local_wide - from_lower.astype(jnp.float32) - from_upper)
        if sweep == SWEEPS - 1:
            total = total + diag_fill
        state = total.astype(jnp.bfloat16)
    kept_rows = jnp.einsum(
        "spk,skj->spj", projection, state, preferred_element_type=jnp.float32
    ).astype(jnp.bfloat16)
    children = jnp.einsum(
        "spj,sqj->spq", kept_rows, projection, preferred_element_type=jnp.float32
    ).astype(jnp.bfloat16)
    wire_rows = kept_points * kept_points // points

    def to_wire(blocks):
        return blocks.reshape(blocks.shape[0], wire_rows, points)

    def from_wire(blocks):
        return blocks.reshape(blocks.shape[0], kept_points, kept_points)

    narrow_bit = lax.axis_index("narrow") % 2
    wide_bit = lax.axis_index("wide") % 2
    narrow_zero = narrow_bit == 0
    wide_zero = wide_bit == 0
    even_slots = children[0::2]
    odd_slots = children[1::2]
    retained = jnp.where(narrow_zero, even_slots, odd_slots)
    outgoing = jnp.where(narrow_zero, odd_slots, even_slots)
    incoming = from_wire(from_partner(to_wire(outgoing), "narrow", 0))
    by_child = jnp.where(
        narrow_zero, jnp.stack([retained, incoming]), jnp.stack([incoming, retained])
    )
    retained_two = jnp.where(wide_zero, by_child[:, 0], by_child[:, 1])
    outgoing_two = jnp.where(wide_zero, by_child[:, 1], by_child[:, 0])
    incoming_two = from_wire(from_partner(to_wire(outgoing_two), "wide", 0))
    gathered = jnp.where(
        wide_zero, jnp.stack([retained_two, incoming_two]), jnp.stack([incoming_two, retained_two])
    )
    blocks = gathered.reshape(4, kept_points, kept_points).astype(jnp.float32)
    quad_eye = jnp.eye(4, dtype=jnp.float32)
    diagonal = jnp.einsum("cij,cd->cidj", blocks, quad_eye).reshape(points, points)
    parent_blocks = (parent_far[0].astype(jnp.float32) + diagonal).astype(jnp.bfloat16)[None]
    return (state, parent_blocks)


def solution(mesh):
    in_specs = (
        P(("wide", "narrow"), None, None),
        P(("wide", "narrow"), None, None),
        P(("wide", "narrow"), None, None),
        P(("wide", "narrow"), None, None),
        P(("wide", "narrow"), None, None),
        P(("wide", "narrow"), None, None),
        P(("wide", "narrow")),
        P(("wide", "narrow")),
    )
    out_specs = (P(("wide", "narrow"), None, None), P(("wide", "narrow"), None, None))
    return jax.shard_map(local, mesh=mesh, in_specs=in_specs, out_specs=out_specs, check_vma=False)
```

profile of v0, /device:TPU:6, one launch (start us, length us, event | category | flops | bytes accessed | tf_op | source)
XLA Modules:
  0.0 128.3 jit_solution(1196548384987585508)
XLA Ops:
  0.6 0.0 copy-start
  1.5 0.7 fusion.28
  2.2 0.1 copy-done
  2.2 0.0 copy-start.1
  2.2 3.5 %fusion.12 = bf16[4,256,256]{2,1,0:T(8,128)(2,1)} fusion(bf16[4,256,512]{2,1,0:T(8,128)(2,1)} %param.9, bf16[4,512,512]{2,1,0:T(8,128)(2,1)S(1)} %copy-done, bf16[4,256,256]{2,1,0:T(8,128)(2,1)} %param.8, f32[4,256]{1,0:T(4,128)S(1)} %fusion.28, f32[4]{0:T(128)S(1)} %compare_convert_fusion), kind=kOutput, calls=%fused_computation.21 | convolution fusion | flops 807403520 | bytes 4198416 | tf_op jit(solution)/shard_map/skr,sjr->skj/dot_general | solution.py:53
  5.8 3.5 %collective-permute-start = (bf16[4,256,256]{2,1,0:T(8,128)(2,1)}, bf16[4,256,256]{2,1,0:T(8,128)(2,1)}, u32[]{:S(2)}, u32[]{:S(2)}) collective-permute-start(bf16[4,256,256]{2,1,0:T(8,128)(2,1)} %fusion.12), channel_id=1, source_target_pairs={{0,8},{8,16},{16,24},{24,32},{32,40},{40,48},{48,56},{56,64},{64,7... | collective-permute-start | bytes 1572872 | tf_op jit(solution)/shard_map/ppermute | solution.py:11
  9.3 0.0 copy-done.1
  9.3 3.5 %collective-permute-start.1 = (bf16[4,256,256]{2,1,0:T(8,128)(2,1)S(1)}, bf16[4,256,256]{2,1,0:T(8,128)(2,1)S(1)}, u32[]{:S(2)}, u32[]{:S(2)}) collective-permute-start(bf16[4,256,256]{2,1,0:T(8,128)(2,1)S(1)} %copy-done.1), channel_id=1, source_target_pairs={{0,8},{8,16},{16,24},{24,32},{32,40},{40,48},{48,56},{56,64},{64,7... | collective-permute-start | bytes 1572872 | tf_op jit(solution)/shard_map/ppermute | solution.py:11
  12.8 10.7 %collective-permute-start.2 = (bf16[4,256,256]{2,1,0:T(8,128)(2,1)}, bf16[4,256,256]{2,1,0:T(8,128)(2,1)}, u32[]{:S(2)}, u32[]{:S(2)}) collective-permute-start(bf16[4,256,256]{2,1,0:T(8,128)(2,1)} %fusion.12), channel_id=1, source_target_pairs={{0,504},{8,0},{16,8},{24,16},{32,24},{40,32},{48,40},{56,48},{64,5... | collective-permute-start | bytes 1572872 | tf_op jit(solution)/shard_map/ppermute | solution.py:11
  23.5 9.2 %collective-permute-done = bf16[4,256,256]{2,1,0:T(8,128)(2,1)} collective-permute-done((bf16[4,256,256]{2,1,0:T(8,128)(2,1)}, bf16[4,256,256]{2,1,0:T(8,128)(2,1)}, u32[]{:S(2)}, u32[]{:S(2)}) %collective-permute-start) | collective-permute-done | bytes 524320 | tf_op jit(solution)/shard_map/ppermute | solution.py:11
  32.7 10.3 %collective-permute-done.1 = bf16[4,256,256]{2,1,0:T(8,128)(2,1)S(1)} collective-permute-done((bf16[4,256,256]{2,1,0:T(8,128)(2,1)S(1)}, bf16[4,256,256]{2,1,0:T(8,128)(2,1)S(1)}, u32[]{:S(2)}, u32[]{:S(2)}) %collective-permute-start.1) | collective-permute-done | bytes 524320 | tf_op jit(solution)/shard_map/ppermute | solution.py:11
  43.0 2.7 %convert_subtract_fusion.3 = f32[4,256,256]{2,1,0:T(8,128)} fusion(bf16[4,256,256]{2,1,0:T(8,128)(2,1)} %fusion.12, bf16[4,256,256]{2,1,0:T(8,128)(2,1)S(1)} %collective-permute-done.1, bf16[4,256,256]{2,1,0:T(8,128)(2,1)} %collective-permute-done), kind=kOutput, calls=%fused_computation.3 | convolution fusion | flops 269746176 | bytes 2621440 | tf_op jit(solution)/shard_map/sji,sjk->sik/dot_general | solution.py:28
  45.7 0.0 collective-permute-done.2
  45.7 2.8 %fusion.13 = bf16[4,256,256]{2,1,0:T(8,128)(2,1)} fusion(f32[4,256,256]{2,1,0:T(8,128)} %convert_subtract_fusion.3, bf16[4,256,256]{2,1,0:T(8,128)(2,1)S(1)} %copy-done.1, bf16[4,256,256]{2,1,0:T(8,128)(2,1)} %collective-permute-done.2, f32[4,256]{1,0:T(4,128)S(1)} %fusion.28, f32[4]{0:T(128)S(1)} %compare_convert_fusion), kind=kOutput, calls=%fused_computation.22 | convolution fusion | flops 270008320 | bytes 2625552 | tf_op jit(solution)/shard_map/sij,sjk->sik/dot_general | solution.py:69
  48.5 1.9 %collective-permute-start.3 = (bf16[4,256,256]{2,1,0:T(8,128)(2,1)}, bf16[4,256,256]{2,1,0:T(8,128)(2,1)}, u32[]{:S(2)}, u32[]{:S(2)}) collective-permute-start(bf16[4,256,256]{2,1,0:T(8,128)(2,1)} %fusion.13), channel_id=1, source_target_pairs={{0,8},{8,16},{16,24},{24,32},{32,40},{40,48},{48,56},{56,64},{64,7... | collective-permute-start | bytes 1572872 | tf_op jit(solution)/shard_map/ppermute | solution.py:11
  50.4 7.2 %collective-permute-start.4 = (bf16[4,256,256]{2,1,0:T(8,128)(2,1)}, bf16[4,256,256]{2,1,0:T(8,128)(2,1)}, u32[]{:S(2)}, u32[]{:S(2)}) collective-permute-start(bf16[4,256,256]{2,1,0:T(8,128)(2,1)} %fusion.13), channel_id=1, source_target_pairs={{0,504},{8,0},{16,8},{24,16},{32,24},{40,32},{48,40},{56,48},{64,5... | collective-permute-start | bytes 1572872 | tf_op jit(solution)/shard_map/ppermute | solution.py:11
  57.7 9.4 %collective-permute-done.3 = bf16[4,256,256]{2,1,0:T(8,128)(2,1)} collective-permute-done((bf16[4,256,256]{2,1,0:T(8,128)(2,1)}, bf16[4,256,256]{2,1,0:T(8,128)(2,1)}, u32[]{:S(2)}, u32[]{:S(2)}) %collective-permute-start.3) | collective-permute-done | bytes 524320 | tf_op jit(solution)/shard_map/ppermute | solution.py:11
  67.1 2.7 %convert_subtract_fusion.2 = f32[4,256,256]{2,1,0:T(8,128)} fusion(bf16[4,256,256]{2,1,0:T(8,128)(2,1)} %fusion.12, bf16[4,256,256]{2,1,0:T(8,128)(2,1)S(1)} %collective-permute-done.1, bf16[4,256,256]{2,1,0:T(8,128)(2,1)} %collective-permute-done.3), kind=kOutput, calls=%fused_computation.2 | convolution fusion | flops 269746176 | bytes 2621440 | tf_op jit(solution)/shard_map/sji,sjk->sik/dot_general | solution.py:28
  69.8 0.0 collective-permute-done.4
  69.8 2.8 %fusion.14 = bf16[4,256,256]{2,1,0:T(8,128)(2,1)} fusion(f32[4,256,256]{2,1,0:T(8,128)} %convert_subtract_fusion.2, bf16[4,256,256]{2,1,0:T(8,128)(2,1)S(1)} %copy-done.1, bf16[4,256,256]{2,1,0:T(8,128)(2,1)} %collective-permute-done.4, f32[4,256]{1,0:T(4,128)S(1)} %fusion.28, f32[4]{0:T(128)S(1)} %compare_convert_fusion), kind=kOutput, calls=%fused_computation.23 | convolution fusion | flops 270008320 | bytes 2625552 | tf_op jit(solution)/shard_map/sij,sjk->sik/dot_general | solution.py:69
  72.6 1.9 %collective-permute-start.5 = (bf16[4,256,256]{2,1,0:T(8,128)(2,1)}, bf16[4,256,256]{2,1,0:T(8,128)(2,1)}, u32[]{:S(2)}, u32[]{:S(2)}) collective-permute-start(bf16[4,256,256]{2,1,0:T(8,128)(2,1)} %fusion.14), channel_id=1, source_target_pairs={{0,8},{8,16},{16,24},{24,32},{32,40},{40,48},{48,56},{56,64},{64,7... | collective-permute-start | bytes 1572872 | tf_op jit(solution)/shard_map/ppermute | solution.py:11
  74.5 7.2 %collective-permute-start.6 = (bf16[4,256,256]{2,1,0:T(8,128)(2,1)}, bf16[4,256,256]{2,1,0:T(8,128)(2,1)}, u32[]{:S(2)}, u32[]{:S(2)}) collective-permute-start(bf16[4,256,256]{2,1,0:T(8,128)(2,1)} %fusion.14), channel_id=1, source_target_pairs={{0,504},{8,0},{16,8},{24,16},{32,24},{40,32},{48,40},{56,48},{64,5... | collective-permute-start | bytes 1572872 | tf_op jit(solution)/shard_map/ppermute | solution.py:11
  81.8 8.6 %collective-permute-done.5 = bf16[4,256,256]{2,1,0:T(8,128)(2,1)} collective-permute-done((bf16[4,256,256]{2,1,0:T(8,128)(2,1)}, bf16[4,256,256]{2,1,0:T(8,128)(2,1)}, u32[]{:S(2)}, u32[]{:S(2)}) %collective-permute-start.5) | collective-permute-done | bytes 524320 | tf_op jit(solution)/shard_map/ppermute | solution.py:11
  90.4 2.7 %convert_subtract_fusion.1 = f32[4,256,256]{2,1,0:T(8,128)} fusion(bf16[4,256,256]{2,1,0:T(8,128)(2,1)} %fusion.12, bf16[4,256,256]{2,1,0:T(8,128)(2,1)S(1)} %collective-permute-done.1, bf16[4,256,256]{2,1,0:T(8,128)(2,1)} %collective-permute-done.5), kind=kOutput, calls=%fused_computation.1 | convolution fusion | flops 269746176 | bytes 2621440 | tf_op jit(solution)/shard_map/sji,sjk->sik/dot_general | solution.py:28
  93.1 0.0 copy-start.5
  93.1 0.0 collective-permute-done.6
  93.1 2.8 %fusion.15 = bf16[4,256,256]{2,1,0:T(8,128)(2,1)} fusion(f32[4,256,256]{2,1,0:T(8,128)} %convert_subtract_fusion.1, bf16[4,256,256]{2,1,0:T(8,128)(2,1)S(1)} %copy-done.1, bf16[4,256,256]{2,1,0:T(8,128)(2,1)} %collective-permute-done.6, f32[4,256]{1,0:T(4,128)S(1)} %fusion.28, f32[4]{0:T(128)S(1)} %compare_convert_fusion), kind=kOutput, calls=%fused_computation.24 | convolution fusion | flops 270008320 | bytes 2625552 | tf_op jit(solution)/shard_map/sij,sjk->sik/dot_general | solution.py:69
  95.9 1.9 %collective-permute-start.7 = (bf16[4,256,256]{2,1,0:T(8,128)(2,1)}, bf16[4,256,256]{2,1,0:T(8,128)(2,1)}, u32[]{:S(2)}, u32[]{:S(2)}) collective-permute-start(bf16[4,256,256]{2,1,0:T(8,128)(2,1)} %fusion.15), channel_id=1, source_target_pairs={{0,8},{8,16},{16,24},{24,32},{32,40},{40,48},{48,56},{56,64},{64,7... | collective-permute-start | bytes 1572872 | tf_op jit(solution)/shard_map/ppermute | solution.py:11
  97.8 0.7 fusion.27
  98.5 7.2 %collective-permute-start.8 = (bf16[4,256,256]{2,1,0:T(8,128)(2,1)}, bf16[4,256,256]{2,1,0:T(8,128)(2,1)}, u32[]{:S(2)}, u32[]{:S(2)}) collective-permute-start(bf16[4,256,256]{2,1,0:T(8,128)(2,1)} %fusion.15), channel_id=1, source_target_pairs={{0,504},{8,0},{16,8},{24,16},{32,24},{40,32},{48,40},{56,48},{64,5... | collective-permute-start | bytes 1572872 | tf_op jit(solution)/shard_map/ppermute | solution.py:11
  105.8 0.0 copy-done.5
  105.8 0.1 select_subtract_fusion
  105.9 6.9 %collective-permute-done.7 = bf16[4,256,256]{2,1,0:T(8,128)(2,1)} collective-permute-done((bf16[4,256,256]{2,1,0:T(8,128)(2,1)}, bf16[4,256,256]{2,1,0:T(8,128)(2,1)}, u32[]{:S(2)}, u32[]{:S(2)}) %collective-permute-start.7) | collective-permute-done | bytes 524320 | tf_op jit(solution)/shard_map/ppermute | solution.py:11
  112.8 2.7 %convert_subtract_fusion = f32[4,256,256]{2,1,0:T(8,128)} fusion(bf16[4,256,256]{2,1,0:T(8,128)(2,1)} %fusion.12, bf16[4,256,256]{2,1,0:T(8,128)(2,1)S(1)} %collective-permute-done.1, bf16[4,256,256]{2,1,0:T(8,128)(2,1)} %collective-permute-done.7), kind=kOutput, calls=%fused_computation | convolution fusion | flops 269746176 | bytes 2621440 | tf_op jit(solution)/shard_map/sji,sjk->sik/dot_general | solution.py:28
  115.5 0.0 copy-start.2
  115.5 0.0 collective-permute-done.8
  115.5 2.1 %fusion.24 = bf16[4,256,256]{2,1,0:T(8,128)(2,1)S(1)} fusion(f32[4,256,256]{2,1,0:T(8,128)} %convert_subtract_fusion, bf16[4,256,256]{2,1,0:T(8,128)(2,1)S(1)} %copy-done.1, bf16[4,256,256]{2,1,0:T(8,128)(2,1)} %collective-permute-done.8, f32[4,256]{1,0:T(4,128)S(1)} %select_subtract_fusion, f32[256,256]{1,0:T(8,128)} %fusion.27, f32[4,256]{1,0:T(4,128)S(1)} %fusion.28, ...), kind=kOutput, calls=%fused_computation.45 | convolution fusion | flops 270532608 | bytes 2891792 | tf_op jit(solution)/shard_map/sij,sjk->sik/dot_general | solution.py:69
  117.5 0.0 copy-done.2
  117.6 0.0 copy-start.3
  117.6 0.0 copy-start.4
  117.6 0.3 fusion.26
  117.9 0.1 reshape.126
  118.0 1.9 %collective-permute-start.9 = (bf16[2,16,256]{2,1,0:T(8,128)(2,1)S(1)}, bf16[2,16,256]{2,1,0:T(8,128)(2,1)S(1)}, u32[]{:S(2)}, u32[]{:S(2)}) collective-permute-start(bf16[2,16,256]{2,1,0:T(8,128)(2,1)S(1)} %reshape.126), channel_id=1, source_target_pairs={{0,1},{1,0},{2,3},{3,2},{4,5},{5,4},{6,7},{7,6},{8,9},{9,8},{10,11... | collective-permute-start | bytes 49160 | tf_op jit(solution)/shard_map/ppermute | solution.py:21
  120.0 1.1 collective-permute-done.9
  121.1 0.1 stack_reshape.8
  121.2 0.1 select_n.75
  121.3 1.9 %collective-permute-start.10 = (bf16[2,16,256]{2,1,0:T(8,128)(2,1)S(1)}, bf16[2,16,256]{2,1,0:T(8,128)(2,1)S(1)}, u32[]{:S(2)}, u32[]{:S(2)}) collective-permute-start(bf16[2,16,256]{2,1,0:T(8,128)(2,1)S(1)} %select_n.75), channel_id=1, source_target_pairs={{0,8},{8,0},{16,24},{24,16},{32,40},{40,32},{48,56},{56,48},{64,72... | collective-permute-start | bytes 49160 | tf_op jit(solution)/shard_map/ppermute | solution.py:21
  123.3 3.7 %collective-permute-done.10 = bf16[2,16,256]{2,1,0:T(8,128)(2,1)S(1)} collective-permute-done((bf16[2,16,256]{2,1,0:T(8,128)(2,1)S(1)}, bf16[2,16,256]{2,1,0:T(8,128)(2,1)S(1)}, u32[]{:S(2)}, u32[]{:S(2)}) %collective-permute-start.10) | collective-permute-done | bytes 16416 | tf_op jit(solution)/shard_map/ppermute | solution.py:21
  127.0 0.1 stack_reshape.9
  127.1 0.2 multiply_bitcast_fusion
  127.3 0.3 reshape.128
  127.6 0.0 copy-done.4
  127.6 0.7 add_convert_fusion
  128.3 0.0 copy-done.3
  (7 shorter events, 0.1 us)
Async XLA Ops:
  0.6 1.6 %copy-start = (bf16[4,512,512]{2,1,0:T(8,128)(2,1)S(1)}, bf16[4,512,512]{2,1,0:T(8,128)(2,1)}, u32[]{:S(2)}) copy-start(bf16[4,512,512]{2,1,0:T(8,128)(2,1)} %param.10) | copy-start | bytes 6291460
  2.2 7.0 %copy-start.1 = (bf16[4,256,256]{2,1,0:T(8,128)(2,1)S(1)}, bf16[4,256,256]{2,1,0:T(8,128)(2,1)}, u32[]{:S(2)}) copy-start(bf16[4,256,256]{2,1,0:T(8,128)(2,1)} %param.11) | copy-start | bytes 1572868
  5.8 26.9 %collective-permute-start = (bf16[4,256,256]{2,1,0:T(8,128)(2,1)}, bf16[4,256,256]{2,1,0:T(8,128)(2,1)}, u32[]{:S(2)}, u32[]{:S(2)}) collective-permute-start(bf16[4,256,256]{2,1,0:T(8,128)(2,1)} %fusion.12), channel_id=1, source_target_pairs={{0,8},{8,16},{16,24},{24,32},{32,40},{40,48},{48,56},{56,64},{64,7... | collective-permute-start | bytes 1572872 | tf_op jit(solution)/shard_map/ppermute | solution.py:11
  9.3 33.7 %collective-permute-start.1 = (bf16[4,256,256]{2,1,0:T(8,128)(2,1)S(1)}, bf16[4,256,256]{2,1,0:T(8,128)(2,1)S(1)}, u32[]{:S(2)}, u32[]{:S(2)}) collective-permute-start(bf16[4,256,256]{2,1,0:T(8,128)(2,1)S(1)} %copy-done.1), channel_id=1, source_target_pairs={{0,8},{8,16},{16,24},{24,32},{32,40},{40,48},{48,56},{56,64},{64,7... | collective-permute-start | bytes 1572872 | tf_op jit(solution)/shard_map/ppermute | solution.py:11
  12.8 32.9 %collective-permute-start.2 = (bf16[4,256,256]{2,1,0:T(8,128)(2,1)}, bf16[4,256,256]{2,1,0:T(8,128)(2,1)}, u32[]{:S(2)}, u32[]{:S(2)}) collective-permute-start(bf16[4,256,256]{2,1,0:T(8,128)(2,1)} %fusion.12), channel_id=1, source_target_pairs={{0,504},{8,0},{16,8},{24,16},{32,24},{40,32},{48,40},{56,48},{64,5... | collective-permute-start | bytes 1572872 | tf_op jit(solution)/shard_map/ppermute | solution.py:11
  48.5 18.6 %collective-permute-start.3 = (bf16[4,256,256]{2,1,0:T(8,128)(2,1)}, bf16[4,256,256]{2,1,0:T(8,128)(2,1)}, u32[]{:S(2)}, u32[]{:S(2)}) collective-permute-start(bf16[4,256,256]{2,1,0:T(8,128)(2,1)} %fusion.13), channel_id=1, source_target_pairs={{0,8},{8,16},{16,24},{24,32},{32,40},{40,48},{48,56},{56,64},{64,7... | collective-permute-start | bytes 1572872 | tf_op jit(solution)/shard_map/ppermute | solution.py:11
  50.4 19.4 %collective-permute-start.4 = (bf16[4,256,256]{2,1,0:T(8,128)(2,1)}, bf16[4,256,256]{2,1,0:T(8,128)(2,1)}, u32[]{:S(2)}, u32[]{:S(2)}) collective-permute-start(bf16[4,256,256]{2,1,0:T(8,128)(2,1)} %fusion.13), channel_id=1, source_target_pairs={{0,504},{8,0},{16,8},{24,16},{32,24},{40,32},{48,40},{56,48},{64,5... | collective-permute-start | bytes 1572872 | tf_op jit(solution)/shard_map/ppermute | solution.py:11
  72.6 17.8 %collective-permute-start.5 = (bf16[4,256,256]{2,1,0:T(8,128)(2,1)}, bf16[4,256,256]{2,1,0:T(8,128)(2,1)}, u32[]{:S(2)}, u32[]{:S(2)}) collective-permute-start(bf16[4,256,256]{2,1,0:T(8,128)(2,1)} %fusion.14), channel_id=1, source_target_pairs={{0,8},{8,16},{16,24},{24,32},{32,40},{40,48},{48,56},{56,64},{64,7... | collective-permute-start | bytes 1572872 | tf_op jit(solution)/shard_map/ppermute | solution.py:11
  74.5 18.6 %collective-permute-start.6 = (bf16[4,256,256]{2,1,0:T(8,128)(2,1)}, bf16[4,256,256]{2,1,0:T(8,128)(2,1)}, u32[]{:S(2)}, u32[]{:S(2)}) collective-permute-start(bf16[4,256,256]{2,1,0:T(8,128)(2,1)} %fusion.14), channel_id=1, source_target_pairs={{0,504},{8,0},{16,8},{24,16},{32,24},{40,32},{48,40},{56,48},{64,5... | collective-permute-start | bytes 1572872 | tf_op jit(solution)/shard_map/ppermute | solution.py:11
  93.1 12.7 %copy-start.5 = (s32[4]{0:T(128)S(1)}, s32[4]{0:T(128)}, u32[]{:S(2)}) copy-start(s32[4]{0:T(128)} %param.14) | copy-start | bytes 52
  95.9 16.9 %collective-permute-start.7 = (bf16[4,256,256]{2,1,0:T(8,128)(2,1)}, bf16[4,256,256]{2,1,0:T(8,128)(2,1)}, u32[]{:S(2)}, u32[]{:S(2)}) collective-permute-start(bf16[4,256,256]{2,1,0:T(8,128)(2,1)} %fusion.15), channel_id=1, source_target_pairs={{0,8},{8,16},{16,24},{24,32},{32,40},{40,48},{48,56},{56,64},{64,7... | collective-permute-start | bytes 1572872 | tf_op jit(solution)/shard_map/ppermute | solution.py:11
  98.5 17.0 %collective-permute-start.8 = (bf16[4,256,256]{2,1,0:T(8,128)(2,1)}, bf16[4,256,256]{2,1,0:T(8,128)(2,1)}, u32[]{:S(2)}, u32[]{:S(2)}) collective-permute-start(bf16[4,256,256]{2,1,0:T(8,128)(2,1)} %fusion.15), channel_id=1, source_target_pairs={{0,504},{8,0},{16,8},{24,16},{32,24},{40,32},{48,40},{56,48},{64,5... | collective-permute-start | bytes 1572872 | tf_op jit(solution)/shard_map/ppermute | solution.py:11
  115.5 2.1 %copy-start.2 = (bf16[4,64,256]{2,1,0:T(8,128)(2,1)S(1)}, bf16[4,64,256]{2,1,0:T(8,128)(2,1)}, u32[]{:S(2)}) copy-start(bf16[4,64,256]{2,1,0:T(8,128)(2,1)} %param.12) | copy-start | bytes 393220
  117.6 10.8 %copy-start.3 = (bf16[4,256,256]{2,1,0:T(8,128)(2,1)}, bf16[4,256,256]{2,1,0:T(8,128)(2,1)S(1)}, u32[]{:S(2)}) copy-start(bf16[4,256,256]{2,1,0:T(8,128)(2,1)S(1)} %fusion.24) | copy-start | bytes 1572868
  117.6 10.1 %copy-start.4 = (bf16[1,256,256]{2,1,0:T(8,128)(2,1)S(1)}, bf16[1,256,256]{2,1,0:T(8,128)(2,1)}, u32[]{:S(2)}) copy-start(bf16[1,256,256]{2,1,0:T(8,128)(2,1)} %param.13) | copy-start | bytes 393220
  118.0 3.1 %collective-permute-start.9 = (bf16[2,16,256]{2,1,0:T(8,128)(2,1)S(1)}, bf16[2,16,256]{2,1,0:T(8,128)(2,1)S(1)}, u32[]{:S(2)}, u32[]{:S(2)}) collective-permute-start(bf16[2,16,256]{2,1,0:T(8,128)(2,1)S(1)} %reshape.126), channel_id=1, source_target_pairs={{0,1},{1,0},{2,3},{3,2},{4,5},{5,4},{6,7},{7,6},{8,9},{9,8},{10,11... | collective-permute-start | bytes 49160 | tf_op jit(solution)/shard_map/ppermute | solution.py:21
  121.3 5.6 %collective-permute-start.10 = (bf16[2,16,256]{2,1,0:T(8,128)(2,1)S(1)}, bf16[2,16,256]{2,1,0:T(8,128)(2,1)S(1)}, u32[]{:S(2)}, u32[]{:S(2)}) collective-permute-start(bf16[2,16,256]{2,1,0:T(8,128)(2,1)S(1)} %select_n.75), channel_id=1, source_target_pairs={{0,8},{8,0},{16,24},{24,16},{32,40},{40,32},{48,56},{56,48},{64,72... | collective-permute-start | bytes 49160 | tf_op jit(solution)/shard_map/ppermute | solution.py:21
where the time goes:
time: 129 us; the launch traced here: 128 us
  waiting for transfers between devices  49.2 us (38%)
  starting transfers between devices  49 us (38%)
  matrix products  25.1 us (19%)
  other arithmetic  2.48 us (2%)
  between operations  1.68 us (1%)
    ppermute x9, starting transfers between devices, shifted(): lax.ppermute(shard, axis, [(i, (i + by) % length) for i in range(length)])  45.1 us
    ppermute x9, waiting for transfers between devices, shifted(): lax.ppermute(shard, axis, [(i, (i + by) % length) for i in range(length)])  44.4 us
    dot_general x4, matrix products, lower_term(): jnp.einsum('sji,sjk->sik', lower_link, lowpart, preferred_element_type=jn...  10.9 us
    dot_general x4, matrix products, local(): jnp.einsum('sij,sjk->sik', link_block, uppart, preferred_element_type=jnp...  10.4 us
    ppermute x2, waiting for transfers between devices, from_partner(): return lax.ppermute(block, axis, route)  4.83 us
    ppermute x2, starting transfers between devices, from_partner(): return lax.ppermute(block, axis, route)  3.82 us
    dot_general x1, matrix products, local(): jnp.einsum('skr,sjr->skj', carried, cross_block, preferred_element_type=j...  3.54 us
  transfers between devices with their start and end apart: 11, of which 7 were waited for; matrix products, arithmetic and copies ran while one was open for 9% of the time, Pallas kernels for 0%

commit v1 on v0

v1 whole, which is shorter than its diff:
```python
import functools

import jax
import jax.numpy as jnp
from jax import lax
from jax.experimental import pallas as pl
from jax.experimental.pallas import tpu as pltpu
from jax.sharding import PartitionSpec as P

SWEEPS = 4
GROUP = 4
MESH = pl.DeviceIdType.MESH
F32 = jnp.float32
BF16 = jnp.bfloat16


def mm(a, b):
    return jnp.dot(a, b, preferred_element_type=F32)


def mm_t(a, b):
    return lax.dot_general(a, b, (((1,), (1,)), ((), ())), preferred_element_type=F32)


def kernel(
    n_wide,
    pc_ref,
    bc_ref,
    self_h,
    cross_h,
    inv_h,
    link_h,
    proj_h,
    far_h,
    out_ref,
    par_ref,
    cross_v,
    inv_v,
    self_v,
    loc_o,
    lnk,
    lnk_m,
    lnk_t,
    st,
    fin,
    rly,
    mo,
    r_m,
    r_s,
    cnt_o,
    cnt_i,
    prj,
    ch_o,
    ch_i,
    far_v,
    ld_sem,
    far_sem,
    own_sem,
    a2a_ss,
    a2a_rs,
    cnt_ss,
    cnt_rs,
    prj_ss,
    prj_rs,
    z_ss,
    z_rs,
    ch_ss,
    ch_rs,
):
    k = self_h.shape[1]
    half = k // 2
    w = lax.axis_index("wide")
    n = lax.axis_index("narrow")
    y = lax.rem(w, GROUP)
    base = w - y
    b = lax.rem(n, 2)
    n0 = n - b
    uy = lax.rem(y + 1, GROUP)
    oy = lax.rem(y + 2, GROUP)
    dy = lax.rem(y + 3, GROUP)
    up = (base + uy, n)
    dn = (base + dy, n)
    op = (base + oy, n)
    zu = (lax.rem(w + GROUP, n_wide), n)
    zd = (lax.rem(w + n_wide - GROUP, n_wide), n)

    def rcopy(src, dst, ssem, rsem, dev):
        return pltpu.make_async_remote_copy(
            src_ref=src,
            dst_ref=dst,
            send_sem=ssem,
            recv_sem=rsem,
            device_id=dev,
            device_id_type=MESH,
        )

    barrier = pltpu.get_barrier_semaphore()
    for i in range(GROUP):
        for c in range(2):
            if i or c:
                dev = (base + lax.rem(y + i, GROUP), n0 + lax.rem(b + c, 2))
                pl.semaphore_signal(barrier, inc=1, device_id=dev, device_id_type=MESH)
    for dev in (zu, zd):
        pl.semaphore_signal(barrier, inc=1, device_id=dev, device_id_type=MESH)

    order = (oy, uy, dy, y)
    loads = []
    for i, slot in enumerate(order):
        trio = []
        for q, (h, v) in enumerate(((cross_h, cross_v), (inv_h, inv_v), (self_h, self_v))):
            cp = pltpu.make_async_copy(h.at[slot], v.at[i], ld_sem.at[i, q])
            cp.start()
            trio.append(cp)
        loads.append(trio)

    live = bc_ref[0]
    effs = []
    for i, slot in enumerate(order):
        eff = jnp.where(slot < live, pc_ref[slot], 0)
        effs.append(eff)
        cnt_o[i] = jnp.full((8, 128), eff, jnp.int32)
    cnt_i[pl.ds(y, 1)] = jnp.full((1, 8, 128), effs[3], jnp.int32)

    def exchange(p, src_op, src_up, src_dn, dst):
        ss, rs = a2a_ss.at[p], a2a_rs.at[p]
        lo, hi = pl.ds(0, half), pl.ds(half, half)
        return (
            rcopy(src_op.at[lo], rly.at[p, 0], ss.at[0], rs.at[0], up),
            rcopy(src_op.at[hi], rly.at[p, 1], ss.at[1], rs.at[1], dn),
            rcopy(src_up, dst.at[y], ss.at[2], rs.at[2], up),
            rcopy(src_dn, dst.at[y], ss.at[3], rs.at[3], dn),
            rcopy(rly.at[p, 0], dst.at[dy, lo], ss.at[4], rs.at[4], up),
            rcopy(rly.at[p, 1], dst.at[uy, hi], ss.at[5], rs.at[5], dn),
        )

    def relay(ex, i):
        ex[i].wait_recv()
        ex[i + 4].start()

    link_x = exchange(0, link_h.at[oy], link_h.at[uy], link_h.at[dy], lnk)
    loc_x = exchange(1, loc_o.at[0], loc_o.at[1], loc_o.at[2], st.at[0])
    fin_x = exchange(2, fin.at[oy], fin.at[uy], fin.at[dy], out_ref)

    pl.semaphore_wait(barrier, 2 * GROUP + 1)

    cnt_x = []
    for i, dev in enumerate((op, up, dn)):
        cp = rcopy(cnt_o.at[i], cnt_i.at[y], cnt_ss.at[i], cnt_rs.at[i], dev)
        cnt_x.append(cp)
    for i in range(4):
        link_x[i].start()
    for cp in cnt_x:
        cp.start()
    own_link = pltpu.make_async_copy(link_h.at[y], lnk.at[y], own_sem.at[0])
    own_link.start()
    own_prj = pltpu.make_async_copy(proj_h.at[y], prj.at[y], own_sem.at[1])
    own_prj.start()
    far_cp = pltpu.make_async_copy(far_h.at[0], far_v, far_sem)
    far_cp.start()

    rows = lax.broadcasted_iota(jnp.int32, (k, k), 0)
    cols = lax.broadcasted_iota(jnp.int32, (k, k), 1)

    def schur(i):
        for cp in loads[i]:
            cp.wait()
        cross = cross_v[i]
        carried = mm(cross, inv_v[i]).astype(BF16)
        update = mm_t(carried, cross)
        inside = (rows < effs[i]) & (cols < effs[i])
        return jnp.where(inside, self_v[i].astype(F32) - update, 0.0).astype(BF16)

    for i in range(3):
        loc_o[i] = schur(i)
    relay(link_x, 0)
    relay(link_x, 1)
    for i in range(4):
        loc_x[i].start()
    st[0, pl.ds(y, 1)] = schur(3)[None]

    own_link.wait()
    for cp in cnt_x:
        cp.wait_recv()
    for i in range(2, 6):
        link_x[i].wait_recv()
    cnts = [cnt_i[j, 0:1, 0:1] for j in range(GROUP)]
    for j in range(GROUP):
        inside = rows < cnts[j]
        if j + 1 < GROUP:
            inside = inside & (cols < cnts[j + 1])
        masked = jnp.where(inside, lnk[j].astype(F32), 0.0)
        lnk_m[j] = masked.astype(BF16)
        lnk_t[j] = masked.T.astype(BF16)

    relay(loc_x, 0)
    relay(loc_x, 1)
    prj_x = []
    for i, (src, dev) in enumerate(((oy, op), (uy, up), (dy, dn))):
        cp = rcopy(proj_h.at[src], prj.at[y], prj_ss.at[i], prj_rs.at[i], dev)
        cp.start()
        prj_x.append(cp)
    for i in range(2, 6):
        loc_x[i].wait_recv()

    def lower(t, j):
        return mm(lnk_t[j], mm(st[t, j], lnk_m[j]).astype(BF16)).astype(BF16)

    def upper(state, j):
        return mm(lnk_m[j], mm(state, lnk_t[j]).astype(BF16))

    def down_copy(t):
        return rcopy(st.at[t, 0], r_s.at[t], z_ss.at[t, 0], z_rs.at[t, 0], zd)

    def up_copy(t):
        return rcopy(mo.at[t], r_m.at[t], z_ss.at[t, 1], z_rs.at[t, 1], zu)

    diag = rows == cols

    def combine(t, j, low, high):
        total = st[0, j].astype(F32) - low.astype(F32) - high
        if t == SWEEPS - 1:
            total = total + jnp.where(diag & (rows >= cnts[j]), 1.0, 0.0)
            fin[j] = total.astype(BF16)
        else:
            st[t + 1, j] = total.astype(BF16)

    own_out = pltpu.make_async_copy(fin.at[y], out_ref.at[y], own_sem.at[2])

    def give_back(j):
        @pl.when(y == j)
        def _():
            own_out.start()

        @pl.when(uy == j)
        def _():
            fin_x[2].start()

        @pl.when(dy == j)
        def _():
            fin_x[3].start()

        @pl.when(oy == j)
        def _():
            fin_x[0].start()
            fin_x[1].start()

    y_half = y // 2
    y_bit = lax.rem(y, 2)
    lane_half = lax.broadcasted_iota(jnp.int32, (1, 2 * prj.shape[1]), 1) // prj.shape[1]

    def child_copies(j):
        c = 2 * (j % 2) + b
        dev = (base + 2 * (j // 2) + y_half, n0 + y_bit)
        mine = (y == 2 * (j // 2) + y_half) & (b == y_bit)
        here = pltpu.make_async_copy(ch_o.at[j], ch_i.at[c], ch_rs.at[c])
        there = rcopy(ch_o.at[j], ch_i.at[c], ch_ss.at[j], ch_rs.at[c], dev)
        return mine, here, there

    def child(j):
        p = prj[j]
        kept = mm(p, fin[j]).astype(BF16)
        both = mm_t(kept, jnp.concatenate([p, p], axis=0))
        ch_o[j] = jnp.where(lane_half == b, both, 0.0).astype(BF16)
        mine, here, there = child_copies(j)

        @pl.when(mine)
        def _():
            here.start()

        @pl.when(jnp.logical_not(mine))
        def _():
            there.start()

    for t in range(SWEEPS):
        last = t == SWEEPS - 1
        down_copy(t).start()
        mo[t] = lower(t, 3)
        up_copy(t).start()
        lows = [lower(t, j) for j in range(3)]
        highs = [upper(st[t, j + 1], j) for j in range(3)]
        combine(t, 1, lows[0], highs[1])
        combine(t, 2, lows[1], highs[2])
        if last:
            give_back(1)
            give_back(2)
            own_prj.wait()
            for cp in prj_x:
                cp.wait_recv()
            child(1)
            child(2)

            @pl.when(y < 2)
            def _():
                relay(fin_x, 0)

            @pl.when(y >= 2)
            def _():
                relay(fin_x, 1)

        down_copy(t).wait_recv()
        combine(t, 3, lows[2], upper(r_s[t], 3))
        if last:
            give_back(3)
        up_copy(t).wait_recv()
        inside = (rows < cnts[0]) & (cols < cnts[0])
        combine(t, 0, jnp.where(inside, r_m[t].astype(F32), 0.0), highs[0])
        if last:
            give_back(0)
            child(3)
            child(0)

    @pl.when(y < 2)
    def _():
        relay(fin_x, 1)

    @pl.when(y >= 2)
    def _():
        relay(fin_x, 0)

    far_cp.wait()
    kp = prj.shape[1]
    for c in range(4):
        pltpu.make_async_copy(ch_o.at[0], ch_i.at[c], ch_rs.at[c]).wait()
        r = pl.ds(kp * c, kp)
        l = pl.ds(2 * kp * (c // 2), 2 * kp)
        far_v[r, l] = (far_v[r, l].astype(F32) + ch_i[c].astype(F32)).astype(BF16)
    par_cp = pltpu.make_async_copy(far_v, par_ref.at[0], far_sem)
    par_cp.start()

    for i in range(2, 6):
        fin_x[i].wait_recv()
    own_out.wait()
    par_cp.wait()
    for ex in (link_x, loc_x, fin_x):
        for cp in ex:
            cp.wait_send()
    for cp in cnt_x + prj_x:
        cp.wait_send()
    for t in range(SWEEPS):
        down_copy(t).wait_send()
        up_copy(t).wait_send()
    for j in range(GROUP):
        mine, _, there = child_copies(j)

        @pl.when(jnp.logical_not(mine))
        def _():
            there.wait_send()


def local(
    n_wide,
    self_block,
    cross_block,
    redundant_inverse,
    link_block,
    projection,
    parent_far,
    point_count,
    box_count,
):
    slots, k, r = cross_block.shape
    kp = projection.shape[1]
    hbm = pl.BlockSpec(memory_space=pl.ANY)
    smem = pl.BlockSpec(memory_space=pltpu.SMEM)
    dma = pltpu.SemaphoreType.DMA
    return pl.pallas_call(
        functools.partial(kernel, n_wide),
        name="skeleton",
        out_shape=(
            jax.ShapeDtypeStruct(self_block.shape, BF16),
            jax.ShapeDtypeStruct(parent_far.shape, BF16),
        ),
        in_specs=[smem, smem] + [hbm] * 6,
        out_specs=(hbm, hbm),
        scratch_shapes=[
            pltpu.VMEM((slots, k, r), BF16),
            pltpu.VMEM((slots, r, r), BF16),
            pltpu.VMEM((slots, k, k), BF16),
            pltpu.VMEM((3, k, k), BF16),
            pltpu.VMEM((GROUP, k, k), BF16),
            pltpu.VMEM((GROUP, k, k), BF16),
            pltpu.VMEM((GROUP, k, k), BF16),
            pltpu.VMEM((SWEEPS, GROUP, k, k), BF16),
            pltpu.VMEM((GROUP, k, k), BF16),
            pltpu.VMEM((3, 2, k // 2, k), BF16),
            pltpu.VMEM((SWEEPS, k, k), BF16),
            pltpu.VMEM((SWEEPS, k, k), BF16),
            pltpu.VMEM((SWEEPS, k, k), BF16),
            pltpu.VMEM((GROUP, 8, 128), jnp.int32),
            pltpu.VMEM((GROUP, 8, 128), jnp.int32),
            pltpu.VMEM((GROUP, kp, k), BF16),
            pltpu.VMEM((GROUP, kp, 2 * kp), BF16),
            pltpu.VMEM((GROUP, kp, 2 * kp), BF16),
            pltpu.VMEM((k, k), BF16),
            dma((4, 3)),
            dma,
            dma((3,)),
            dma((3, 6)),
            dma((3, 6)),
            dma((3,)),
            dma((3,)),
            dma((3,)),
            dma((3,)),
            dma((SWEEPS, 2)),
            dma((SWEEPS, 2)),
            dma((GROUP,)),
            dma((GROUP,)),
        ],
        compiler_params=pltpu.CompilerParams(
            collective_id=0, has_side_effects=True, vmem_limit_bytes=48 * 1024 * 1024
        ),
    )(
        point_count,
        box_count,
        self_block,
        cross_block,
        redundant_inverse,
        link_block,
        projection,
        parent_far,
    )


def solution(mesh):
    block = P(("wide", "narrow"), None, None)
    flat = P(("wide", "narrow"))
    return jax.shard_map(
        functools.partial(local, mesh.shape["wide"]),
        mesh=mesh,
        in_specs=(block,) * 6 + (flat,) * 2,
        out_specs=(block, block),
        check_vma=False,
    )
```

time: 129 us -> 68.8 us (0.53)
  Pallas kernels: 0 us -> 58.3 us
  waiting for transfers between devices: 49.2 us -> 0 us
  starting transfers between devices: 49 us -> 0 us
  matrix products: 25.1 us -> 0 us
  local copies, waits for them, and re-layouts: 0.82 us -> 8.8 us
  other arithmetic: 2.48 us -> 0 us
    pallas_call x0 -> x1, Pallas kernels: none -> 58.3 us  [local(): pl.pallas_call(functools.partial(kernel, n_wide), name='skeleton', out_sh...]
    ppermute x11 -> x0, waiting for transfers between devices: 49.2 us -> none  [the longest x9 44.4 us: shifted(): lax.ppermute(shard, axis, [(i, (i + by) % length) for i in range(length)])]
    ppermute x11 -> x0, starting transfers between devices: 49 us -> none  [the longest x9 45.1 us: shifted(): lax.ppermute(shard, axis, [(i, (i + by) % length) for i in range(length)])]
    dot_general x10 -> x0, matrix products: 25.1 us -> none  [the longest x4 10.9 us: lower_term(): jnp.einsum('sji,sjk->sik', lower_link, lowpart, preferred_element_type=jn...]
    unnamed x12 -> x16, local copies, waits for them, and re-layouts: 0.1 us -> 8.8 us
    convert_element_type x4 -> x0, other arithmetic: 2.15 us -> none  [the longest x1 0.74 us: local(): identity = jnp.eye(points, dtype=jnp.float32)]
  transfers between devices with their start and end apart: 11 -> 0, of which waited for: 7 -> 0; matrix products, arithmetic and copies ran while one was open for 9% -> 0% of each run, Pallas kernels for 0% -> 0%
where the time goes in v1:
time: 68.8 us; the launch traced here: 68.4 us
  Pallas kernels  58.3 us (85%)
  local copies, waits for them, and re-layouts  8.8 us (13%)
  between operations  1.3 us (2%)
    pallas_call x1, Pallas kernels, local(): pl.pallas_call(functools.partial(kernel, n_wide), name='skeleton', out_sh...  58.3 us
    unnamed x16, local copies, waits for them, and re-layouts  8.8 us

profile of v1, /device:TPU:6, one launch (start us, length us, event | category | flops | bytes accessed | tf_op | source)
XLA Modules:
  0.0 68.4 jit_solution(15125766111345321403)
XLA Ops:
  1.3 0.0 copy-start
  1.3 1.6 %copy-done = bf16[4,512,512]{2,1,0:T(8,128)(2,1)S(1)} copy-done((bf16[4,512,512]{2,1,0:T(8,128)(2,1)S(1)}, bf16[4,512,512]{2,1,0:T(8,128)(2,1)}, u32[]{:S(2)}) %copy-start) | copy-done | bytes 2097176
  2.9 0.0 copy-start.1
  2.9 1.2 %copy-done.1 = bf16[4,256,512]{2,1,0:T(8,128)(2,1)S(1)} copy-done((bf16[4,256,512]{2,1,0:T(8,128)(2,1)S(1)}, bf16[4,256,512]{2,1,0:T(8,128)(2,1)}, u32[]{:S(2)}) %copy-start.1) | copy-done | bytes 1048600
  4.1 0.0 copy-start.2
  4.1 1.0 %copy-done.2 = bf16[4,256,256]{2,1,0:T(8,128)(2,1)S(1)} copy-done((bf16[4,256,256]{2,1,0:T(8,128)(2,1)S(1)}, bf16[4,256,256]{2,1,0:T(8,128)(2,1)}, u32[]{:S(2)}) %copy-start.2) | copy-done | bytes 524312
  5.1 0.0 copy-start.3
  5.1 1.0 %copy-done.3 = bf16[4,256,256]{2,1,0:T(8,128)(2,1)S(1)} copy-done((bf16[4,256,256]{2,1,0:T(8,128)(2,1)S(1)}, bf16[4,256,256]{2,1,0:T(8,128)(2,1)}, u32[]{:S(2)}) %copy-start.3) | copy-done | bytes 524312
  6.2 0.0 copy-start.4
  6.2 0.9 %copy-done.4 = bf16[4,64,256]{2,1,0:T(8,128)(2,1)S(1)} copy-done((bf16[4,64,256]{2,1,0:T(8,128)(2,1)S(1)}, bf16[4,64,256]{2,1,0:T(8,128)(2,1)}, u32[]{:S(2)}) %copy-start.4) | copy-done | bytes 131096
  7.1 0.0 copy-start.5
  7.1 0.9 %copy-done.5 = bf16[1,256,256]{2,1,0:T(8,128)(2,1)S(1)} copy-done((bf16[1,256,256]{2,1,0:T(8,128)(2,1)S(1)}, bf16[1,256,256]{2,1,0:T(8,128)(2,1)}, u32[]{:S(2)}) %copy-start.5) | copy-done | bytes 131096
  8.0 0.0 copy-start.6
  8.0 0.7 copy-done.6
  8.6 58.3 %skeleton.1 = (bf16[4,256,256]{2,1,0:T(8,128)(2,1)S(1)}, bf16[1,256,256]{2,1,0:T(8,128)(2,1)S(1)}) custom-call(s32[4]{0:T(128)S(1)} %copy-done.6, s32[1]{0:T(128)S(6)} %copy.12.bc_ref, bf16[4,256,256]{2,1,0:T(8,128)(2,1)S(1)} %copy-done.2, bf16[4,256,512]{2,1,0:T(8,128)(2,1)S(1)} %copy-done.1, bf16[4,512,512]{2,1,0:T(8,128)(2,1)S(1)} %copy-done, ...), custom_call_target="tpu_custom_call" | custom-call | tf_op jit(solution)/shard_map/skeleton/pallas_call | solution.py:366
  67.0 0.8 %copy.13 = bf16[4,256,256]{2,1,0:T(8,128)(2,1)} copy(bf16[4,256,256]{2,1,0:T(8,128)(2,1)S(1)} %get-tuple-element.4) | data formatting | bytes 1048576
  67.8 0.7 copy.14
Async XLA Ops:
  1.3 1.6 %copy-start = (bf16[4,512,512]{2,1,0:T(8,128)(2,1)S(1)}, bf16[4,512,512]{2,1,0:T(8,128)(2,1)}, u32[]{:S(2)}) copy-start(bf16[4,512,512]{2,1,0:T(8,128)(2,1)} %inv_h.1) | copy-start | bytes 6291460
  2.9 1.2 %copy-start.1 = (bf16[4,256,512]{2,1,0:T(8,128)(2,1)S(1)}, bf16[4,256,512]{2,1,0:T(8,128)(2,1)}, u32[]{:S(2)}) copy-start(bf16[4,256,512]{2,1,0:T(8,128)(2,1)} %cross_h.1) | copy-start | bytes 3145732
  4.1 1.0 %copy-start.2 = (bf16[4,256,256]{2,1,0:T(8,128)(2,1)S(1)}, bf16[4,256,256]{2,1,0:T(8,128)(2,1)}, u32[]{:S(2)}) copy-start(bf16[4,256,256]{2,1,0:T(8,128)(2,1)} %self_h.1) | copy-start | bytes 1572868
  5.1 1.0 %copy-start.3 = (bf16[4,256,256]{2,1,0:T(8,128)(2,1)S(1)}, bf16[4,256,256]{2,1,0:T(8,128)(2,1)}, u32[]{:S(2)}) copy-start(bf16[4,256,256]{2,1,0:T(8,128)(2,1)} %link_h.1) | copy-start | bytes 1572868
  6.2 0.9 %copy-start.4 = (bf16[4,64,256]{2,1,0:T(8,128)(2,1)S(1)}, bf16[4,64,256]{2,1,0:T(8,128)(2,1)}, u32[]{:S(2)}) copy-start(bf16[4,64,256]{2,1,0:T(8,128)(2,1)} %proj_h.1) | copy-start | bytes 393220
  7.1 0.9 %copy-start.5 = (bf16[1,256,256]{2,1,0:T(8,128)(2,1)S(1)}, bf16[1,256,256]{2,1,0:T(8,128)(2,1)}, u32[]{:S(2)}) copy-start(bf16[1,256,256]{2,1,0:T(8,128)(2,1)} %far_h.1) | copy-start | bytes 393220
  8.0 0.7 copy-start.6

commit v2 on v1

v2 whole, which is shorter than its diff:
```python
import functools

import jax
import jax.numpy as jnp
from jax import lax
from jax.experimental import pallas as pl
from jax.experimental.pallas import tpu as pltpu
from jax.sharding import PartitionSpec as P

SWEEPS = 4
GROUP = 4
MESH = pl.DeviceIdType.MESH
F32 = jnp.float32
BF16 = jnp.bfloat16


def mm(a, b):
    return jnp.dot(a, b, preferred_element_type=F32)


def mm_t(a, b):
    return lax.dot_general(a, b, (((1,), (1,)), ((), ())), preferred_element_type=F32)


def kernel(
    n_wide,
    pc_h,
    bc_ref,
    self_h,
    cross_h,
    inv_h,
    link_h,
    proj_h,
    far_h,
    out_ref,
    par_ref,
    pc_ref,
    cross_v,
    inv_v,
    self_v,
    loc_o,
    lnk,
    lnk_m,
    lnk_t,
    st,
    fin,
    rly,
    mo,
    r_m,
    r_s,
    cnt_o,
    cnt_i,
    prj,
    ch_o,
    ch_i,
    far_v,
    cnt_ld,
    ld_sem,
    far_sem,
    own_sem,
    a2a_ss,
    a2a_rs,
    cnt_ss,
    cnt_rs,
    prj_ss,
    prj_rs,
    z_ss,
    z_rs,
    ch_ss,
    ch_rs,
):
    k = self_h.shape[1]
    half = k // 2
    w = lax.axis_index("wide")
    n = lax.axis_index("narrow")
    y = lax.rem(w, GROUP)
    base = w - y
    b = lax.rem(n, 2)
    n0 = n - b
    q = y // 2
    uy = lax.rem(y + 1, GROUP)
    oy = lax.rem(y + 2, GROUP)
    dy = lax.rem(y + 3, GROUP)

    def at_z(by):
        return lax.rem(base + n_wide + GROUP * by, n_wide)

    def flag(condition):
        return jnp.where(condition, 1, 0)

    up = (base + uy, n)
    dn = (base + dy, n)
    op = (base + oy, n)
    zu = (at_z(1) + y, n)
    zd = (at_z(-1) + y, n)
    to_up = (at_z(-flag(y == 0)) + uy, n)
    to_dn = (at_z(flag(y == 3)) + dy, n)
    of_up_z = at_z(-flag(y == 2))
    of_dn_z = at_z(flag(y == 1))
    of_up = (of_up_z + uy, n)
    of_dn = (of_dn_z + dy, n)

    def rcopy(src, dst, ssem, rsem, dev):
        return pltpu.make_async_remote_copy(
            src_ref=src,
            dst_ref=dst,
            send_sem=ssem,
            recv_sem=rsem,
            device_id=dev,
            device_id_type=MESH,
        )

    barrier = pltpu.get_barrier_semaphore()

    def greet(dev):
        pl.semaphore_signal(barrier, inc=1, device_id=dev, device_id_type=MESH)

    y_bit = lax.rem(y, 2)
    pair_base = at_z(2 * y_bit - 1) + y + 1 - 2 * y_bit
    for i in range(GROUP):
        for c in range(2):
            if i or c:
                greet((base + lax.rem(y + i, GROUP), n0 + lax.rem(b + c, 2)))
    greet(zu)
    greet(zd)
    greet((pair_base, n0))
    greet((pair_base, n0 + 1))

    order = (uy, dy, oy, y)
    loads = []
    for i, slot in enumerate(order):
        trio = []
        for c, (h, v) in enumerate(((cross_h, cross_v), (inv_h, inv_v), (self_h, self_v))):
            cp = pltpu.make_async_copy(h.at[slot], v.at[i], ld_sem.at[i, c])
            cp.start()
            trio.append(cp)
        loads.append(trio)
        if i == 0:
            pc_cp = pltpu.make_async_copy(pc_h, pc_ref, cnt_ld)
            pc_cp.start()

    lo, hi = pl.ds(0, half), pl.ds(half, half)

    def exchange(p, src_op, dst_op, dst_relay_up, dst_relay_dn, a, bb):
        ss, rs = a2a_ss.at[p], a2a_rs.at[p]
        return (
            rcopy(src_op.at[lo], rly.at[p, 0], ss.at[0], rs.at[0], up),
            rcopy(src_op.at[hi], rly.at[p, 1], ss.at[1], rs.at[1], dn),
            rcopy(a[0], a[1], ss.at[2], rs.at[2], a[2]),
            rcopy(bb[0], bb[1], ss.at[3], rs.at[3], bb[2]),
            rcopy(rly.at[p, 0], dst_relay_up.at[lo], ss.at[4], rs.at[4], up),
            rcopy(rly.at[p, 1], dst_relay_dn.at[hi], ss.at[5], rs.at[5], dn),
        )

    def outward(p, src_up, src_dn, src_op, dst):
        return exchange(
            p,
            src_op,
            dst.at[2],
            dst.at[2],
            dst.at[2],
            (src_up, dst.at[3], to_up),
            (src_dn, dst.at[1], to_dn),
        )

    link_x = outward(0, link_h.at[uy], link_h.at[dy], link_h.at[oy], lnk)
    loc_x = outward(1, loc_o.at[0], loc_o.at[1], loc_o.at[2], st.at[0])
    fin_x = exchange(
        2,
        fin.at[2],
        out_ref.at[y],
        out_ref.at[dy],
        out_ref.at[uy],
        (fin.at[1], out_ref.at[y], of_up),
        (fin.at[3], out_ref.at[y], of_dn),
    )

    def relay(ex, i):
        ex[i].wait_recv()
        ex[i + 4].start()

    pl.semaphore_wait(barrier, 2 * GROUP + 3)
    link_x[2].start()
    link_x[3].start()
    own_link = pltpu.make_async_copy(link_h.at[y], lnk.at[0], own_sem.at[0])
    own_link.start()
    own_prj = pltpu.make_async_copy(proj_h.at[y], prj.at[0], own_sem.at[1])
    own_prj.start()
    far_cp = pltpu.make_async_copy(far_h.at[0], far_v, far_sem)
    far_cp.start()

    pc_cp.wait()
    live = bc_ref[0]
    effs = []
    for i, slot in enumerate(order):
        eff = jnp.where(slot < live, pc_ref[slot], 0)
        effs.append(eff)
        if i < 3:
            cnt_o[i] = jnp.full((8, 128), eff, jnp.int32)
        else:
            cnt_i[0] = jnp.full((8, 128), eff, jnp.int32)

    rows = lax.broadcasted_iota(jnp.int32, (k, k), 0)
    cols = lax.broadcasted_iota(jnp.int32, (k, k), 1)

    def schur(i):
        for cp in loads[i]:
            cp.wait()
        cross = cross_v[i]
        carried = mm(cross, inv_v[i]).astype(BF16)
        update = mm_t(carried, cross)
        inside = (rows < effs[i]) & (cols < effs[i])
        return jnp.where(inside, self_v[i].astype(F32) - update, 0.0).astype(BF16)

    loc_o[0] = schur(0)
    loc_o[1] = schur(1)
    loc_x[2].start()
    loc_x[3].start()
    cnt_x = []
    for i, (rel, dev) in enumerate(((3, to_up), (1, to_dn), (2, op))):
        cp = rcopy(cnt_o.at[i], cnt_i.at[rel], cnt_ss.at[i], cnt_rs.at[i], dev)
        cp.start()
        cnt_x.append(cp)
    loc_o[2] = schur(2)
    link_x[0].start()
    link_x[1].start()
    loc_x[0].start()
    loc_x[1].start()
    st[0, 0] = schur(3)

    def origin(j):
        return lax.rem(q + j, GROUP)

    own_link.wait()
    for cp in cnt_x:
        cp.wait_recv()

    def count(j):
        return cnt_i[pl.ds(origin(j), 1), 0:1, 0:1][0]

    def prepare(j, last):
        inside = rows < count(j)
        if not last:
            inside = inside & (cols < count(j + 1))
        masked = jnp.where(inside, lnk[pl.ds(origin(j), 1)][0].astype(F32), 0.0)
        lnk_m[pl.ds(j, 1)] = masked.astype(BF16)[None]
        lnk_t[pl.ds(j, 1)] = masked.T.astype(BF16)[None]

    def state(t, j):
        if t == 0:
            return st[0, pl.ds(origin(j), 1)][0]
        return st[t, j]

    def lower(t, j):
        return mm(lnk_t[j], mm(state(t, j), lnk_m[j]).astype(BF16)).astype(BF16)

    def upper(above, j):
        return mm(lnk_m[j], mm(above, lnk_t[j]).astype(BF16))

    def down_copy(t):
        src = st.at[t, origin(0)] if t == 0 else st.at[t, 0]
        return rcopy(src, r_s.at[t], z_ss.at[t, 0], z_rs.at[t, 0], zd)

    def up_copy(t):
        return rcopy(mo.at[t], r_m.at[t], z_ss.at[t, 1], z_rs.at[t, 1], zu)

    def send_halo(t):
        down_copy(t).start()
        mo[t] = lower(t, 3)
        up_copy(t).start()

    def when_type(i, copies):
        for v in range(2):

            @pl.when(q == v)
            def _():
                copies[i + (v if i == 2 else -v)].wait_recv()

    when_type(2, link_x)
    prepare(3, True)
    prepare(0, False)
    when_type(2, loc_x)
    send_halo(0)
    when_type(3, link_x)
    prepare(1 + q, False)
    relay(link_x, 0)
    relay(link_x, 1)
    relay(loc_x, 0)
    relay(loc_x, 1)
    prj_x = []
    for i, (src, rel, dev) in enumerate(((uy, 3, to_up), (dy, 1, to_dn), (oy, 2, op))):
        cp = rcopy(proj_h.at[src], prj.at[rel], prj_ss.at[i], prj_rs.at[i], dev)
        cp.start()
        prj_x.append(cp)
    for i in (4, 5):
        link_x[i].wait_recv()
    prepare(2 - q, False)
    when_type(3, loc_x)
    for i in (4, 5):
        loc_x[i].wait_recv()

    def combine(t, j, low, high):
        own = state(0, j)
        total = own.astype(F32) - low.astype(F32) - high
        if t == SWEEPS - 1:
            total = total + jnp.where((rows == cols) & (rows >= count(j)), 1.0, 0.0)
            fin[pl.ds(origin(j), 1)] = total.astype(BF16)[None]
        else:
            st[t + 1, j] = total.astype(BF16)

    own_out = pltpu.make_async_copy(fin.at[0], out_ref.at[y], own_sem.at[2])
    kp = prj.shape[1]
    lane_half = lax.broadcasted_iota(jnp.int32, (1, 2 * kp), 1) // kp

    def child_copies(rel):
        from_y = lax.rem(y + rel, GROUP)
        from_base = (base, of_up_z, base, of_dn_z)[rel]
        c = 2 * lax.rem(from_y, 2) + b
        owner_y = 2 * (from_y // 2) + q
        dev = (from_base + owner_y, n0 + y_bit)
        mine = (from_base == base) & (owner_y == y) & (b == y_bit)
        here = pltpu.make_async_copy(ch_o.at[rel], ch_i.at[c], ch_rs.at[c])
        there = rcopy(ch_o.at[rel], ch_i.at[c], ch_ss.at[rel], ch_rs.at[c], dev)
        return mine, here, there

    def child(rel):
        p = prj[rel]
        kept = mm(p, fin[rel]).astype(BF16)
        both = mm_t(kept, jnp.concatenate([p, p], axis=0))
        ch_o[rel] = jnp.where(lane_half == b, both, 0.0).astype(BF16)
        mine, here, there = child_copies(rel)

        @pl.when(mine)
        def _():
            here.start()

        @pl.when(jnp.logical_not(mine))
        def _():
            there.start()

    for t in range(SWEEPS):
        last = t == SWEEPS - 1
        if t:
            send_halo(t)
        lows = [lower(t, j) for j in range(3)]
        highs = [upper(state(t, j + 1), j) for j in range(3)]
        combine(t, 1, lows[0], highs[1])
        combine(t, 2, lows[1], highs[2])
        if last:
            fin_x[0].start()
            fin_x[1].start()

            @pl.when(q == 0)
            def _():
                fin_x[2].start()

            @pl.when(q == 1)
            def _():
                fin_x[3].start()

            own_prj.wait()
            for cp in prj_x:
                cp.wait_recv()
            child(2)

            @pl.when(q == 0)
            def _():
                child(1)

            @pl.when(q == 1)
            def _():
                child(3)

            relay(fin_x, 0)
            relay(fin_x, 1)

        down_copy(t).wait_recv()
        combine(t, 3, lows[2], upper(r_s[t], 3))
        up_copy(t).wait_recv()
        inside = (rows < count(0)) & (cols < count(0))
        combine(t, 0, jnp.where(inside, r_m[t].astype(F32), 0.0), highs[0])

    own_out.start()

    @pl.when(q == 0)
    def _():
        fin_x[3].start()
        child(3)

    @pl.when(q == 1)
    def _():
        fin_x[2].start()
        child(1)

    child(0)
    far_cp.wait()
    for c in range(4):
        pltpu.make_async_copy(ch_o.at[0], ch_i.at[c], ch_rs.at[c]).wait()
        r = pl.ds(kp * c, kp)
        l = pl.ds(2 * kp * (c // 2), 2 * kp)
        far_v[r, l] = (far_v[r, l].astype(F32) + ch_i[c].astype(F32)).astype(BF16)
    par_cp = pltpu.make_async_copy(far_v, par_ref.at[0], far_sem)
    par_cp.start()

    for i in range(2, 6):
        fin_x[i].wait_recv()
    own_out.wait()
    par_cp.wait()
    for ex in (link_x, loc_x, fin_x):
        for cp in ex:
            cp.wait_send()
    for cp in cnt_x + prj_x:
        cp.wait_send()
    for t in range(SWEEPS):
        down_copy(t).wait_send()
        up_copy(t).wait_send()
    for rel in range(GROUP):
        mine, _, there = child_copies(rel)

        @pl.when(jnp.logical_not(mine))
        def _():
            there.wait_send()


def local(
    n_wide,
    self_block,
    cross_block,
    redundant_inverse,
    link_block,
    projection,
    parent_far,
    point_count,
    box_count,
):
    slots, k, r = cross_block.shape
    kp = projection.shape[1]
    hbm = pl.BlockSpec(memory_space=pl.ANY)
    smem = pl.BlockSpec(memory_space=pltpu.SMEM)
    dma = pltpu.SemaphoreType.DMA
    return pl.pallas_call(
        functools.partial(kernel, n_wide),
        name="skeleton",
        out_shape=(
            jax.ShapeDtypeStruct(self_block.shape, BF16),
            jax.ShapeDtypeStruct(parent_far.shape, BF16),
        ),
        in_specs=[hbm, smem] + [hbm] * 6,
        out_specs=(hbm, hbm),
        scratch_shapes=[
            pltpu.SMEM((slots,), jnp.int32),
            pltpu.VMEM((slots, k, r), BF16),
            pltpu.VMEM((slots, r, r), BF16),
            pltpu.VMEM((slots, k, k), BF16),
            pltpu.VMEM((3, k, k), BF16),
            pltpu.VMEM((GROUP, k, k), BF16),
            pltpu.VMEM((GROUP, k, k), BF16),
            pltpu.VMEM((GROUP, k, k), BF16),
            pltpu.VMEM((SWEEPS, GROUP, k, k), BF16),
            pltpu.VMEM((GROUP, k, k), BF16),
            pltpu.VMEM((3, 2, k // 2, k), BF16),
            pltpu.VMEM((SWEEPS, k, k), BF16),
            pltpu.VMEM((SWEEPS, k, k), BF16),
            pltpu.VMEM((SWEEPS, k, k), BF16),
            pltpu.VMEM((GROUP, 8, 128), jnp.int32),
            pltpu.VMEM((GROUP, 8, 128), jnp.int32),
            pltpu.VMEM((GROUP, kp, k), BF16),
            pltpu.VMEM((GROUP, kp, 2 * kp), BF16),
            pltpu.VMEM((GROUP, kp, 2 * kp), BF16),
            pltpu.VMEM((k, k), BF16),
            dma,
            dma((4, 3)),
            dma,
            dma((3,)),
            dma((3, 6)),
            dma((3, 6)),
            dma((3,)),
            dma((3,)),
            dma((3,)),
            dma((3,)),
            dma((SWEEPS, 2)),
            dma((SWEEPS, 2)),
            dma((GROUP,)),
            dma((GROUP,)),
        ],
        compiler_params=pltpu.CompilerParams(
            collective_id=0, has_side_effects=True, vmem_limit_bytes=48 * 1024 * 1024
        ),
    )(
        pltpu.with_memory_space_constraint(point_count, pltpu.HBM),
        box_count,
        *(
            pltpu.with_memory_space_constraint(x, pltpu.HBM)
            for x in (
                self_block,
                cross_block,
                redundant_inverse,
                link_block,
                projection,
                parent_far,
            )
        ),
    )


def solution(mesh):
    block = P(("wide", "narrow"), None, None)
    flat = P(("wide", "narrow"))
    return jax.shard_map(
        functools.partial(local, mesh.shape["wide"]),
        mesh=mesh,
        in_specs=(block,) * 6 + (flat,) * 2,
        out_specs=(block, block),
        check_vma=False,
    )
```

time: 68.8 us -> 55.5 us (0.81)
  the two profiles are of different devices: /device:TPU:6 before, /device:TPU:1 now
where the time goes in v2:
time: 55.5 us; the launch traced here: 55.4 us
  Pallas kernels  52.7 us (95%)
  local copies, waits for them, and re-layouts  1.45 us (3%)
  between operations  1.29 us (2%)
    pallas_call x1, Pallas kernels, local(): pl.pallas_call(functools.partial(kernel, n_wide), name='skeleton', out_sh...  52.7 us
    unnamed x2, local copies, waits for them, and re-layouts  1.45 us

profile of v2, /device:TPU:1, one launch (start us, length us, event | category | flops | bytes accessed | tf_op | source)
XLA Modules:
  0.0 55.4 jit_solution(3823650466065661633)
XLA Ops:
  1.3 52.7 %skeleton.1 = (bf16[4,256,256]{2,1,0:T(8,128)(2,1)S(1)}, bf16[1,256,256]{2,1,0:T(8,128)(2,1)S(1)}) custom-call(s32[4]{0:T(128)} %pc_h.1, s32[1]{0:T(128)S(6)} %copy.12.bc_ref, bf16[4,256,256]{2,1,0:T(8,128)(2,1)} %self_h.1, bf16[4,256,512]{2,1,0:T(8,128)(2,1)} %cross_h.1, bf16[4,512,512]{2,1,0:T(8,128)(2,1)} %inv_h.1, bf16[4,256,256]{2,1,0:T(8,128)(2,1)} %link_h.1, ...), custom_call_target="tpu_custom_call" | custom-call | tf_op jit(solution)/shard_map/skeleton/pallas_call | solution.py:441
  53.9 0.8 %copy.13 = bf16[4,256,256]{2,1,0:T(8,128)(2,1)} copy(bf16[4,256,256]{2,1,0:T(8,128)(2,1)S(1)} %get-tuple-element.4) | data formatting | bytes 1048576
  54.7 0.7 %copy.14 = bf16[1,256,256]{2,1,0:T(8,128)(2,1)} copy(bf16[1,256,256]{2,1,0:T(8,128)(2,1)S(1)} %get-tuple-element.5) | data formatting | bytes 262144

commit v3 on v2

--- a/solution.py
+++ b/solution.py
@@ -179,16 +179,6 @@
         ex[i].wait_recv()
         ex[i + 4].start()
 
-    pl.semaphore_wait(barrier, 2 * GROUP + 3)
-    link_x[2].start()
-    link_x[3].start()
-    own_link = pltpu.make_async_copy(link_h.at[y], lnk.at[0], own_sem.at[0])
-    own_link.start()
-    own_prj = pltpu.make_async_copy(proj_h.at[y], prj.at[0], own_sem.at[1])
-    own_prj.start()
-    far_cp = pltpu.make_async_copy(far_h.at[0], far_v, far_sem)
-    far_cp.start()
-
     pc_cp.wait()
     live = bc_ref[0]
     effs = []
@@ -200,6 +190,21 @@
         else:
             cnt_i[0] = jnp.full((8, 128), eff, jnp.int32)
 
+    pl.semaphore_wait(barrier, 2 * GROUP + 3)
+    cnt_x = []
+    for i, (rel, dev) in enumerate(((3, to_up), (1, to_dn), (2, op))):
+        cp = rcopy(cnt_o.at[i], cnt_i.at[rel], cnt_ss.at[i], cnt_rs.at[i], dev)
+        cp.start()
+        cnt_x.append(cp)
+    link_x[2].start()
+    link_x[3].start()
+    own_link = pltpu.make_async_copy(link_h.at[y], lnk.at[0], own_sem.at[0])
+    own_link.start()
+    own_prj = pltpu.make_async_copy(proj_h.at[y], prj.at[0], own_sem.at[1])
+    own_prj.start()
+    far_cp = pltpu.make_async_copy(far_h.at[0], far_v, far_sem)
+    far_cp.start()
+
     rows = lax.broadcasted_iota(jnp.int32, (k, k), 0)
     cols = lax.broadcasted_iota(jnp.int32, (k, k), 1)
 
@@ -216,17 +221,12 @@
     loc_o[1] = schur(1)
     loc_x[2].start()
     loc_x[3].start()
-    cnt_x = []
-    for i, (rel, dev) in enumerate(((3, to_up), (1, to_dn), (2, op))):
-        cp = rcopy(cnt_o.at[i], cnt_i.at[rel], cnt_ss.at[i], cnt_rs.at[i], dev)
-        cp.start()
-        cnt_x.append(cp)
     loc_o[2] = schur(2)
+    st[0, 0] = schur(3)
+    for i in (2, 3):
+        link_x[i].wait_send()
     link_x[0].start()
     link_x[1].start()
-    loc_x[0].start()
-    loc_x[1].start()
-    st[0, 0] = schur(3)
 
     def origin(j):
         return lax.rem(q + j, GROUP)
@@ -247,15 +247,16 @@
         lnk_t[pl.ds(j, 1)] = masked.T.astype(BF16)[None]
 
     def state(t, j):
-        if t == 0:
-            return st[0, pl.ds(origin(j), 1)][0]
-        return st[t, j]
+        return st[t, pl.ds(origin(j) if t == 0 else j, 1)][0]
+
+    def at(ref, j):
+        return ref[pl.ds(j, 1)][0]
 
     def lower(t, j):
-        return mm(lnk_t[j], mm(state(t, j), lnk_m[j]).astype(BF16)).astype(BF16)
+        return mm(at(lnk_t, j), mm(state(t, j), at(lnk_m, j)).astype(BF16)).astype(BF16)
 
     def upper(above, j):
-        return mm(lnk_m[j], mm(above, lnk_t[j]).astype(BF16))
+        return mm(at(lnk_m, j), mm(above, at(lnk_t, j)).astype(BF16))
 
     def down_copy(t):
         src = st.at[t, origin(0)] if t == 0 else st.at[t, 0]
@@ -264,11 +265,6 @@
     def up_copy(t):
         return rcopy(mo.at[t], r_m.at[t], z_ss.at[t, 1], z_rs.at[t, 1], zu)
 
-    def send_halo(t):
-        down_copy(t).start()
-        mo[t] = lower(t, 3)
-        up_copy(t).start()
-
     def when_type(i, copies):
         for v in range(2):
 
@@ -279,29 +275,32 @@
     when_type(2, link_x)
     prepare(3, True)
     prepare(0, False)
+    for i in (2, 3):
+        loc_x[i].wait_send()
+    loc_x[0].start()
+    loc_x[1].start()
+    relay(link_x, 0)
+    relay(link_x, 1)
     when_type(2, loc_x)
-    send_halo(0)
+    down_copy(0).start()
+    mo[0] = lower(0, 3)
+    up_copy(0).start()
     when_type(3, link_x)
     prepare(1 + q, False)
-    relay(link_x, 0)
-    relay(link_x, 1)
     relay(loc_x, 0)
     relay(loc_x, 1)
-    prj_x = []
-    for i, (src, rel, dev) in enumerate(((uy, 3, to_up), (dy, 1, to_dn), (oy, 2, op))):
-        cp = rcopy(proj_h.at[src], prj.at[rel], prj_ss.at[i], prj_rs.at[i], dev)
-        cp.start()
-        prj_x.append(cp)
     for i in (4, 5):
         link_x[i].wait_recv()
     prepare(2 - q, False)
     when_type(3, loc_x)
+    down_copy(0).wait_recv()
+    top = upper(r_s[0], 3)
+    up_copy(0).wait_recv()
     for i in (4, 5):
         loc_x[i].wait_recv()
 
     def combine(t, j, low, high):
-        own = state(0, j)
-        total = own.astype(F32) - low.astype(F32) - high
+        total = state(0, j).astype(F32) - low.astype(F32) - high
         if t == SWEEPS - 1:
             total = total + jnp.where((rows == cols) & (rows >= count(j)), 1.0, 0.0)
             fin[pl.ds(origin(j), 1)] = total.astype(BF16)[None]
@@ -314,7 +313,7 @@
 
     def child_copies(rel):
         from_y = lax.rem(y + rel, GROUP)
-        from_base = (base, of_up_z, base, of_dn_z)[rel]
+        from_base = jnp.where(rel == 1, of_up_z, jnp.where(rel == 3, of_dn_z, base))
         c = 2 * lax.rem(from_y, 2) + b
         owner_y = 2 * (from_y // 2) + q
         dev = (from_base + owner_y, n0 + y_bit)
@@ -324,10 +323,10 @@
         return mine, here, there
 
     def child(rel):
-        p = prj[rel]
-        kept = mm(p, fin[rel]).astype(BF16)
+        p = at(prj, rel)
+        kept = mm(p, at(fin, rel)).astype(BF16)
         both = mm_t(kept, jnp.concatenate([p, p], axis=0))
-        ch_o[rel] = jnp.where(lane_half == b, both, 0.0).astype(BF16)
+        ch_o[pl.ds(rel, 1)] = jnp.where(lane_half == b, both, 0.0).astype(BF16)[None]
         mine, here, there = child_copies(rel)
 
         @pl.when(mine)
@@ -338,61 +337,86 @@
         def _():
             there.start()
 
-    for t in range(SWEEPS):
-        last = t == SWEEPS - 1
-        if t:
-            send_halo(t)
-        lows = [lower(t, j) for j in range(3)]
-        highs = [upper(state(t, j + 1), j) for j in range(3)]
-        combine(t, 1, lows[0], highs[1])
-        combine(t, 2, lows[1], highs[2])
-        if last:
-            fin_x[0].start()
-            fin_x[1].start()
-
-            @pl.when(q == 0)
-            def _():
-                fin_x[2].start()
-
-            @pl.when(q == 1)
-            def _():
-                fin_x[3].start()
-
-            own_prj.wait()
-            for cp in prj_x:
-                cp.wait_recv()
-            child(2)
-
-            @pl.when(q == 0)
-            def _():
-                child(1)
-
-            @pl.when(q == 1)
-            def _():
-                child(3)
-
-            relay(fin_x, 0)
-            relay(fin_x, 1)
-
+    def halo_low(t):
+        inside = (rows < count(0)) & (cols < count(0))
+        return jnp.where(inside, r_m[t].astype(F32), 0.0)
+
+    def bottom_done(t, high):
+        combine(t, 0, halo_low(t), high)
+        down_copy(t + 1).start()
+
+    def top_done(t, low, high):
+        combine(t, 3, low, high)
+        mo[t + 1] = lower(t + 1, 3)
+        up_copy(t + 1).start()
+
+    bottom_done(0, upper(state(0, 1), 0))
+    top_done(0, lower(0, 2), top)
+    prj_x = []
+    for i, (src, rel, dev) in enumerate(((uy, 3, to_up), (dy, 1, to_dn), (oy, 2, op))):
+        cp = rcopy(proj_h.at[src], prj.at[rel], prj_ss.at[i], prj_rs.at[i], dev)
+        cp.start()
+        prj_x.append(cp)
+    combine(0, 1, lower(0, 0), upper(state(0, 2), 1))
+    combine(0, 2, lower(0, 1), upper(state(0, 3), 2))
+    for t in range(1, SWEEPS - 1):
+        combine(t, 1, lower(t, 0), upper(st[t, 2], 1))
+        combine(t, 2, lower(t, 1), upper(st[t, 3], 2))
+        low = lower(t, 2)
+        high = upper(st[t, 1], 0)
         down_copy(t).wait_recv()
-        combine(t, 3, lows[2], upper(r_s[t], 3))
+        combine(t, 3, low, upper(r_s[t], 3))
         up_copy(t).wait_recv()
-        inside = (rows < count(0)) & (cols < count(0))
-        combine(t, 0, jnp.where(inside, r_m[t].astype(F32), 0.0), highs[0])
-
-    own_out.start()
+        combine(t, 0, halo_low(t), high)
+        down_copy(t + 1).start()
+        mo[t + 1] = lower(t + 1, 3)
+        up_copy(t + 1).start()
+    t = SWEEPS - 1
+    far_pos = 2 - q
+    near_pos = 1 + q
+    combine(t, far_pos, lower(t, far_pos - 1), upper(state(t, far_pos + 1), far_pos))
+    fin_x[0].start()
+    fin_x[1].start()
+    combine(t, near_pos, lower(t, near_pos - 1), upper(state(t, near_pos + 1), near_pos))
+    low = lower(t, 2)
+    high = upper(st[t, 1], 0)
+    own_prj.wait()
+    for cp in prj_x:
+        cp.wait_recv()
+    for i in (0, 1):
+        fin_x[i].wait_send()
+
+    def give_back(early):
+        @pl.when(q == (0 if early else 1))
+        def _():
+            fin_x[2].start()
+
+        @pl.when(q == (1 if early else 0))
+        def _():
+            fin_x[3].start()
+
+    give_back(True)
+    child(origin(1))
+    child(origin(2))
+    relay(fin_x, 0)
+    relay(fin_x, 1)
+    down_copy(t).wait_recv()
+    combine(t, 3, low, upper(r_s[t], 3))
+    child(origin(3))
 
     @pl.when(q == 0)
     def _():
         fin_x[3].start()
-        child(3)
+
+    up_copy(t).wait_recv()
+    combine(t, 0, halo_low(t), high)
+    child(origin(0))
 
     @pl.when(q == 1)
     def _():
         fin_x[2].start()
-        child(1)
-
-    child(0)
+
+    own_out.start()
     far_cp.wait()
     for c in range(4):
         pltpu.make_async_copy(ch_o.at[0], ch_i.at[c], ch_rs.at[c]).wait()
@@ -406,9 +430,9 @@
         fin_x[i].wait_recv()
     own_out.wait()
     par_cp.wait()
-    for ex in (link_x, loc_x, fin_x):
-        for cp in ex:
-            cp.wait_send()
+    for ex, left in ((link_x, (0, 1, 4, 5)), (loc_x, (0, 1, 4, 5)), (fin_x, (2, 3, 4, 5))):
+        for i in left:
+            ex[i].wait_send()
     for cp in cnt_x + prj_x:
         cp.wait_send()
     for t in range(SWEEPS):
@@ -420,6 +444,17 @@
         @pl.when(jnp.logical_not(mine))
         def _():
             there.wait_send()
+
+
+def settle(out_v, par_v, out_h, par_h, sem):
+    copies = (
+        pltpu.make_async_copy(out_v, out_h, sem.at[0]),
+        pltpu.make_async_copy(par_v, par_h, sem.at[1]),
+    )
+    for cp in copies:
+        cp.start()
+    for cp in copies:
+        cp.wait()
 
 
 def local(
@@ -438,13 +473,14 @@
     hbm = pl.BlockSpec(memory_space=pl.ANY)
     smem = pl.BlockSpec(memory_space=pltpu.SMEM)
     dma = pltpu.SemaphoreType.DMA
-    return pl.pallas_call(
+    shapes = (
+        jax.ShapeDtypeStruct(self_block.shape, BF16),
+        jax.ShapeDtypeStruct(parent_far.shape, BF16),
+    )
+    results = pl.pallas_call(
         functools.partial(kernel, n_wide),
         name="skeleton",
-        out_shape=(
-            jax.ShapeDtypeStruct(self_block.shape, BF16),
-            jax.ShapeDtypeStruct(parent_far.shape, BF16),
-        ),
+        out_shape=shapes,
         in_specs=[hbm, smem] + [hbm] * 6,
         out_specs=(hbm, hbm),
         scratch_shapes=[
@@ -501,6 +537,14 @@
             )
         ),
     )
+    return pl.pallas_call(
+        settle,
+        name="settle",
+        out_shape=shapes,
+        in_specs=[hbm] * 2,
+        out_specs=(hbm, hbm),
+        scratch_shapes=[dma((2,))],
+    )(*(pltpu.with_memory_space_constraint(x, pltpu.VMEM) for x in results))
 
 
 def solution(mesh):

time: 55.5 us -> 52.8 us (0.951)
  the two profiles are of different devices: /device:TPU:1 before, /device:TPU:6 now
where the time goes in v3:
time: 52.8 us; the launch traced here: 52.6 us
  Pallas kernels  51.3 us (97%)
  between operations  1.29 us (2%)
    pallas_call x1, Pallas kernels, local(): pl.pallas_call(functools.partial(kernel, n_wide), name='skeleton', out_sh...  50.5 us

profile of v3, /device:TPU:6, one launch (start us, length us, event | category | flops | bytes accessed | tf_op | source)
XLA Modules:
  0.0 52.6 jit_solution(7833017544954607764)
XLA Ops:
  1.3 50.5 %skeleton.1 = (bf16[4,256,256]{2,1,0:T(8,128)(2,1)S(1)}, bf16[1,256,256]{2,1,0:T(8,128)(2,1)S(1)}) custom-call(s32[4]{0:T(128)} %pc_h.1, s32[1]{0:T(128)S(6)} %copy.10.bc_ref, bf16[4,256,256]{2,1,0:T(8,128)(2,1)} %self_h.1, bf16[4,256,512]{2,1,0:T(8,128)(2,1)} %cross_h.1, bf16[4,512,512]{2,1,0:T(8,128)(2,1)} %inv_h.1, bf16[4,256,256]{2,1,0:T(8,128)(2,1)} %link_h.1, ...), custom_call_target="tpu_custom_call" | custom-call | tf_op jit(solution)/shard_map/skeleton/pallas_call | solution.py:480
  51.8 0.8 %settle.1 = (bf16[4,256,256]{2,1,0:T(8,128)(2,1)}, bf16[1,256,256]{2,1,0:T(8,128)(2,1)}) custom-call(bf16[4,256,256]{2,1,0:T(8,128)(2,1)S(1)} %get-tuple-element.4.out_v, bf16[1,256,256]{2,1,0:T(8,128)(2,1)S(1)} %get-tuple-element.5.par_v), custom_call_target="tpu_custom_call" | custom-call | tf_op jit(solution)/shard_map/settle/pallas_call | solution.py:540

commit v4 on v3

--- a/solution.py
+++ b/solution.py
@@ -54,6 +54,11 @@
     ch_o,
     ch_i,
     far_v,
+    edge_m,
+    edge_t,
+    edge_loc,
+    edge_sum,
+    edge_cnt,
     cnt_ld,
     ld_sem,
     far_sem,
@@ -68,6 +73,10 @@
     z_rs,
     ch_ss,
     ch_rs,
+    last_ss,
+    last_rs,
+    edge_ss,
+    edge_rs,
 ):
     k = self_h.shape[1]
     half = k // 2
@@ -173,6 +182,14 @@
         out_ref.at[uy],
         (fin.at[1], out_ref.at[y], of_up),
         (fin.at[3], out_ref.at[y], of_dn),
+    )
+
+    last_lo, last_hi = (
+        [
+            rcopy(fin.at[o, part], out_ref.at[y, part], last_ss.at[i], last_rs.at[v, i], dev)
+            for v, (o, dev) in enumerate(((3, of_dn), (1, of_up)))
+        ]
+        for i, part in enumerate((lo, hi))
     )
 
     def relay(ex, i):
@@ -222,11 +239,10 @@
     loc_x[2].start()
     loc_x[3].start()
     loc_o[2] = schur(2)
+    for ex in (link_x, loc_x):
+        ex[0].start()
+        ex[1].start()
     st[0, 0] = schur(3)
-    for i in (2, 3):
-        link_x[i].wait_send()
-    link_x[0].start()
-    link_x[1].start()
 
     def origin(j):
         return lax.rem(q + j, GROUP)
@@ -259,7 +275,7 @@
         return mm(at(lnk_m, j), mm(above, at(lnk_t, j)).astype(BF16))
 
     def down_copy(t):
-        src = st.at[t, origin(0)] if t == 0 else st.at[t, 0]
+        src = st.at[0, origin(0)] if t == 0 else st.at[2, 1] if t == 3 else st.at[t, 0]
         return rcopy(src, r_s.at[t], z_ss.at[t, 0], z_rs.at[t, 0], zd)
 
     def up_copy(t):
@@ -275,16 +291,26 @@
     when_type(2, link_x)
     prepare(3, True)
     prepare(0, False)
-    for i in (2, 3):
-        loc_x[i].wait_send()
-    loc_x[0].start()
-    loc_x[1].start()
-    relay(link_x, 0)
-    relay(link_x, 1)
+    edge_x = [
+        rcopy(src, dst, edge_ss.at[i], edge_rs.at[i], dev)
+        for i, (src, dst, dev) in enumerate(
+            (
+                (lnk_m.at[3], edge_m.at[0], zu),
+                (lnk_m.at[0], edge_m.at[1], zd),
+                (cnt_i.at[origin(0)], edge_cnt, zd),
+                (st.at[0, origin(3)], edge_loc, zu),
+            )
+        )
+    ]
+    for i in range(3):
+        edge_x[i].start()
     when_type(2, loc_x)
     down_copy(0).start()
     mo[0] = lower(0, 3)
     up_copy(0).start()
+    edge_x[3].start()
+    relay(link_x, 0)
+    relay(link_x, 1)
     when_type(3, link_x)
     prepare(1 + q, False)
     relay(loc_x, 0)
@@ -296,9 +322,6 @@
     down_copy(0).wait_recv()
     top = upper(r_s[0], 3)
     up_copy(0).wait_recv()
-    for i in (4, 5):
-        loc_x[i].wait_recv()
-
     def combine(t, j, low, high):
         total = state(0, j).astype(F32) - low.astype(F32) - high
         if t == SWEEPS - 1:
@@ -337,12 +360,12 @@
         def _():
             there.start()
 
-    def halo_low(t):
+    def halo_low(term):
         inside = (rows < count(0)) & (cols < count(0))
-        return jnp.where(inside, r_m[t].astype(F32), 0.0)
+        return jnp.where(inside, term.astype(F32), 0.0)
 
     def bottom_done(t, high):
-        combine(t, 0, halo_low(t), high)
+        combine(t, 0, halo_low(r_m[t]), high)
         down_copy(t + 1).start()
 
     def top_done(t, low, high):
@@ -350,8 +373,25 @@
         mo[t + 1] = lower(t + 1, 3)
         up_copy(t + 1).start()
 
-    bottom_done(0, upper(state(0, 1), 0))
-    top_done(0, lower(0, 2), top)
+    @pl.when(q == 0)
+    def _():
+        bottom_done(0, upper(state(0, 1), 0))
+
+    @pl.when(q == 1)
+    def _():
+        top_done(0, lower(0, 2), top)
+
+    for i in (4, 5):
+        loc_x[i].wait_recv()
+
+    @pl.when(q == 0)
+    def _():
+        top_done(0, lower(0, 2), top)
+
+    @pl.when(q == 1)
+    def _():
+        bottom_done(0, upper(state(0, 1), 0))
+
     prj_x = []
     for i, (src, rel, dev) in enumerate(((uy, 3, to_up), (dy, 1, to_dn), (oy, 2, op))):
         cp = rcopy(proj_h.at[src], prj.at[rel], prj_ss.at[i], prj_rs.at[i], dev)
@@ -359,18 +399,35 @@
         prj_x.append(cp)
     combine(0, 1, lower(0, 0), upper(state(0, 2), 1))
     combine(0, 2, lower(0, 1), upper(state(0, 3), 2))
-    for t in range(1, SWEEPS - 1):
-        combine(t, 1, lower(t, 0), upper(st[t, 2], 1))
-        combine(t, 2, lower(t, 1), upper(st[t, 3], 2))
-        low = lower(t, 2)
-        high = upper(st[t, 1], 0)
-        down_copy(t).wait_recv()
-        combine(t, 3, low, upper(r_s[t], 3))
-        up_copy(t).wait_recv()
-        combine(t, 0, halo_low(t), high)
-        down_copy(t + 1).start()
-        mo[t + 1] = lower(t + 1, 3)
-        up_copy(t + 1).start()
+    combine(1, 1, lower(1, 0), upper(st[1, 2], 1))
+    combine(1, 2, lower(1, 1), upper(st[1, 3], 2))
+    low = lower(1, 2)
+    high = upper(st[1, 1], 0)
+    down_copy(1).wait_recv()
+    combine(1, 3, low, upper(r_s[1], 3))
+    up_copy(1).wait_recv()
+    combine(1, 0, halo_low(r_m[1]), high)
+    down_copy(2).start()
+    down_copy(3).start()
+    mo[2] = lower(2, 3)
+    up_copy(2).start()
+    mo[3] = lower(2, 2)
+    up_copy(3).start()
+    combine(2, 1, lower(2, 0), upper(st[2, 2], 1))
+    combine(2, 2, lower(2, 1), upper(st[2, 3], 2))
+    for cp in edge_x:
+        cp.wait_recv()
+    for i in range(2):
+        edge_t[i] = edge_m[i].astype(F32).T.astype(BF16)
+    edge_high = mm(edge_m[0], mm(st[2, 0], edge_t[0]).astype(BF16))
+    edge_sum[0] = edge_loc[...].astype(F32) - edge_high
+    edge_inside = (rows < edge_cnt[0:1, 0:1]) & (cols < edge_cnt[0:1, 0:1])
+    edge_sum[1] = r_s[0].astype(F32) - jnp.where(edge_inside, mo[2].astype(F32), 0.0)
+    high = upper(st[2, 1], 0)
+    down_copy(2).wait_recv()
+    combine(2, 3, mo[3], upper(r_s[2], 3))
+    up_copy(2).wait_recv()
+    combine(2, 0, halo_low(r_m[2]), high)
     t = SWEEPS - 1
     far_pos = 2 - q
     near_pos = 1 + q
@@ -378,45 +435,47 @@
     fin_x[0].start()
     fin_x[1].start()
     combine(t, near_pos, lower(t, near_pos - 1), upper(state(t, near_pos + 1), near_pos))
+
+    @pl.when(q == 0)
+    def _():
+        fin_x[2].start()
+
+    @pl.when(q == 1)
+    def _():
+        fin_x[3].start()
+
     low = lower(t, 2)
     high = upper(st[t, 1], 0)
     own_prj.wait()
     for cp in prj_x:
         cp.wait_recv()
-    for i in (0, 1):
-        fin_x[i].wait_send()
-
-    def give_back(early):
-        @pl.when(q == (0 if early else 1))
-        def _():
-            fin_x[2].start()
-
-        @pl.when(q == (1 if early else 0))
-        def _():
-            fin_x[3].start()
-
-    give_back(True)
     child(origin(1))
     child(origin(2))
+    down_copy(t).wait_recv()
+    above = edge_sum[1] - mm(edge_m[1], mm(r_s[t], edge_t[1]).astype(BF16))
+    combine(t, 3, low, upper(above.astype(BF16), 3))
+
+    @pl.when(q == 0)
+    def _():
+        last_lo[0].start()
+        child(3)
+        last_hi[0].start()
+
+    up_copy(t).wait_recv()
+    below = (edge_sum[0] - r_m[t].astype(F32)).astype(BF16)
+    below_low = mm(edge_t[0], mm(below, edge_m[0]).astype(BF16)).astype(BF16)
+    combine(t, 0, halo_low(below_low), high)
+
+    @pl.when(q == 1)
+    def _():
+        last_lo[1].start()
+        child(1)
+        last_hi[1].start()
+
+    child(0)
+    own_out.start()
     relay(fin_x, 0)
     relay(fin_x, 1)
-    down_copy(t).wait_recv()
-    combine(t, 3, low, upper(r_s[t], 3))
-    child(origin(3))
-
-    @pl.when(q == 0)
-    def _():
-        fin_x[3].start()
-
-    up_copy(t).wait_recv()
-    combine(t, 0, halo_low(t), high)
-    child(origin(0))
-
-    @pl.when(q == 1)
-    def _():
-        fin_x[2].start()
-
-    own_out.start()
     far_cp.wait()
     for c in range(4):
         pltpu.make_async_copy(ch_o.at[0], ch_i.at[c], ch_rs.at[c]).wait()
@@ -426,14 +485,37 @@
     par_cp = pltpu.make_async_copy(far_v, par_ref.at[0], far_sem)
     par_cp.start()
 
-    for i in range(2, 6):
+    for i in (4, 5):
         fin_x[i].wait_recv()
+    outer = (y == 0) | (y == GROUP - 1)
+
+    @pl.when(outer)
+    def _():
+        for i in range(2):
+            last_lo[i].wait_recv()
+            last_hi[i].wait_recv()
+
+    @pl.when(jnp.logical_not(outer))
+    def _():
+        fin_x[2].wait_recv()
+        fin_x[3].wait_recv()
+
     own_out.wait()
     par_cp.wait()
-    for ex, left in ((link_x, (0, 1, 4, 5)), (loc_x, (0, 1, 4, 5)), (fin_x, (2, 3, 4, 5))):
+    for ex, left in ((link_x, range(6)), (loc_x, range(6)), (fin_x, (0, 1, 4, 5))):
         for i in left:
             ex[i].wait_send()
+    for v in range(2):
+
+        @pl.when(q == v)
+        def _():
+            fin_x[2 + v].wait_send()
+            last_lo[v].wait_send()
+            last_hi[v].wait_send()
+
     for cp in cnt_x + prj_x:
+        cp.wait_send()
+    for cp in edge_x:
         cp.wait_send()
     for t in range(SWEEPS):
         down_copy(t).wait_send()
@@ -504,6 +586,11 @@
             pltpu.VMEM((GROUP, kp, 2 * kp), BF16),
             pltpu.VMEM((GROUP, kp, 2 * kp), BF16),
             pltpu.VMEM((k, k), BF16),
+            pltpu.VMEM((2, k, k), BF16),
+            pltpu.VMEM((2, k, k), BF16),
+            pltpu.VMEM((k, k), BF16),
+            pltpu.VMEM((2, k, k), F32),
+            pltpu.VMEM((8, 128), jnp.int32),
             dma,
             dma((4, 3)),
             dma,
@@ -518,6 +605,10 @@
             dma((SWEEPS, 2)),
             dma((GROUP,)),
             dma((GROUP,)),
+            dma((2,)),
+            dma((2, 2)),
+            dma((4,)),
+            dma((4,)),
         ],
         compiler_params=pltpu.CompilerParams(
             collective_id=0, has_side_effects=True, vmem_limit_bytes=48 * 1024 * 1024

time: 52.8 us -> 50.5 us (0.956)
  Pallas kernels: 51.3 us -> 49.1 us
    pallas_call x1, Pallas kernels: 50.5 us -> 48.3 us  [local(): pl.pallas_call(functools.partial(kernel, n_wide), name='skeleton', out_sh...]
where the time goes in v4:
time: 50.5 us; the launch traced here: 50.4 us
  Pallas kernels  49.1 us (97%)
  between operations  1.29 us (3%)
    pallas_call x1, Pallas kernels, local(): pl.pallas_call(functools.partial(kernel, n_wide), name='skeleton', out_sh...  48.3 us

profile of v4, /device:TPU:6, one launch (start us, length us, event | category | flops | bytes accessed | tf_op | source)
XLA Modules:
  0.0 50.4 jit_solution(6645805846082581450)
XLA Ops:
  1.3 48.3 %skeleton.1 = (bf16[4,256,256]{2,1,0:T(8,128)(2,1)S(1)}, bf16[1,256,256]{2,1,0:T(8,128)(2,1)S(1)}) custom-call(s32[4]{0:T(128)} %pc_h.1, s32[1]{0:T(128)S(6)} %copy.10.bc_ref, bf16[4,256,256]{2,1,0:T(8,128)(2,1)} %self_h.1, bf16[4,256,512]{2,1,0:T(8,128)(2,1)} %cross_h.1, bf16[4,512,512]{2,1,0:T(8,128)(2,1)} %inv_h.1, bf16[4,256,256]{2,1,0:T(8,128)(2,1)} %link_h.1, ...), custom_call_target="tpu_custom_call" | custom-call | tf_op jit(solution)/shard_map/skeleton/pallas_call | solution.py:562
  49.6 0.8 %settle.1 = (bf16[4,256,256]{2,1,0:T(8,128)(2,1)}, bf16[1,256,256]{2,1,0:T(8,128)(2,1)}) custom-call(bf16[4,256,256]{2,1,0:T(8,128)(2,1)S(1)} %get-tuple-element.4.out_v, bf16[1,256,256]{2,1,0:T(8,128)(2,1)S(1)} %get-tuple-element.5.par_v), custom_call_target="tpu_custom_call" | custom-call | tf_op jit(solution)/shard_map/settle/pallas_call | solution.py:631

commit v5 on v4

--- a/solution.py
+++ b/solution.py
@@ -9,6 +9,7 @@
 
 SWEEPS = 4
 GROUP = 4
+PIECES = 2
 MESH = pl.DeviceIdType.MESH
 F32 = jnp.float32
 BF16 = jnp.bfloat16
@@ -67,13 +68,10 @@
     a2a_rs,
     cnt_ss,
     cnt_rs,
-    prj_ss,
     prj_rs,
     z_ss,
     z_rs,
-    ch_ss,
     ch_rs,
-    last_ss,
     last_rs,
     edge_ss,
     edge_rs,
@@ -151,15 +149,22 @@
     lo, hi = pl.ds(0, half), pl.ds(half, half)
 
     def exchange(p, src_op, dst_op, dst_relay_up, dst_relay_dn, a, bb):
-        ss, rs = a2a_ss.at[p], a2a_rs.at[p]
-        return (
-            rcopy(src_op.at[lo], rly.at[p, 0], ss.at[0], rs.at[0], up),
-            rcopy(src_op.at[hi], rly.at[p, 1], ss.at[1], rs.at[1], dn),
-            rcopy(a[0], a[1], ss.at[2], rs.at[2], a[2]),
-            rcopy(bb[0], bb[1], ss.at[3], rs.at[3], bb[2]),
-            rcopy(rly.at[p, 0], dst_relay_up.at[lo], ss.at[4], rs.at[4], up),
-            rcopy(rly.at[p, 1], dst_relay_dn.at[hi], ss.at[5], rs.at[5], dn),
-        )
+        ss, rs = a2a_ss.at[p % 2], a2a_rs.at[p]
+        first, second = [], []
+        for i in range(2 * PIECES):
+            way, piece = i % 2, i // 2
+            rows_of = pl.ds(way * half + piece * (half // PIECES), half // PIECES)
+            held = rly.at[p, way, pl.ds(piece * (half // PIECES), half // PIECES)]
+            dev, dst = ((up, dst_relay_up), (dn, dst_relay_dn))[way]
+            first.append(rcopy(src_op.at[rows_of], held, ss.at[2 + i], rs.at[2 + i], dev))
+            o = 2 + 2 * PIECES + i
+            second.append(rcopy(held, dst.at[rows_of], ss.at[2 + i], rs.at[o], dev))
+        return {
+            2: rcopy(a[0], a[1], ss.at[0], rs.at[0], a[2]),
+            3: rcopy(bb[0], bb[1], ss.at[1], rs.at[1], bb[2]),
+            "first": first,
+            "second": second,
+        }
 
     def outward(p, src_up, src_dn, src_op, dst):
         return exchange(
@@ -186,15 +191,17 @@
 
     last_lo, last_hi = (
         [
-            rcopy(fin.at[o, part], out_ref.at[y, part], last_ss.at[i], last_rs.at[v, i], dev)
+            rcopy(fin.at[o, part], out_ref.at[y, part], a2a_ss.at[1, i], last_rs.at[v, i], dev)
             for v, (o, dev) in enumerate(((3, of_dn), (1, of_up)))
         ]
         for i, part in enumerate((lo, hi))
     )
 
-    def relay(ex, i):
-        ex[i].wait_recv()
-        ex[i + 4].start()
+    def relay(ex):
+        for a, b_ in zip(ex["first"], ex["second"]):
+            a.wait_recv()
+            a.wait_send()
+            b_.start()
 
     pc_cp.wait()
     live = bc_ref[0]
@@ -240,8 +247,8 @@
     loc_x[3].start()
     loc_o[2] = schur(2)
     for ex in (link_x, loc_x):
-        ex[0].start()
-        ex[1].start()
+        for cp in ex["first"]:
+            cp.start()
     st[0, 0] = schur(3)
 
     def origin(j):
@@ -276,10 +283,10 @@
 
     def down_copy(t):
         src = st.at[0, origin(0)] if t == 0 else st.at[2, 1] if t == 3 else st.at[t, 0]
-        return rcopy(src, r_s.at[t], z_ss.at[t, 0], z_rs.at[t, 0], zd)
+        return rcopy(src, r_s.at[t], z_ss.at[t % 2, 0], z_rs.at[t, 0], zd)
 
     def up_copy(t):
-        return rcopy(mo.at[t], r_m.at[t], z_ss.at[t, 1], z_rs.at[t, 1], zu)
+        return rcopy(mo.at[t], r_m.at[t], z_ss.at[t % 2, 1], z_rs.at[t, 1], zu)
 
     def when_type(i, copies):
         for v in range(2):
@@ -302,21 +309,20 @@
             )
         )
     ]
-    for i in range(3):
-        edge_x[i].start()
+    edge_x[0].start()
     when_type(2, loc_x)
     down_copy(0).start()
     mo[0] = lower(0, 3)
     up_copy(0).start()
     edge_x[3].start()
-    relay(link_x, 0)
-    relay(link_x, 1)
+    edge_x[1].start()
+    edge_x[2].start()
+    relay(link_x)
     when_type(3, link_x)
     prepare(1 + q, False)
-    relay(loc_x, 0)
-    relay(loc_x, 1)
-    for i in (4, 5):
-        link_x[i].wait_recv()
+    relay(loc_x)
+    for cp in link_x["second"]:
+        cp.wait_recv()
     prepare(2 - q, False)
     when_type(3, loc_x)
     down_copy(0).wait_recv()
@@ -342,16 +348,19 @@
         dev = (from_base + owner_y, n0 + y_bit)
         mine = (from_base == base) & (owner_y == y) & (b == y_bit)
         here = pltpu.make_async_copy(ch_o.at[rel], ch_i.at[c], ch_rs.at[c])
-        there = rcopy(ch_o.at[rel], ch_i.at[c], ch_ss.at[rel], ch_rs.at[c], dev)
+        there = rcopy(ch_o.at[rel], ch_i.at[c], a2a_ss.at[1, 2 + rel], ch_rs.at[c], dev)
         return mine, here, there
 
-    def child(rel):
-        p = at(prj, rel)
-        kept = mm(p, at(fin, rel)).astype(BF16)
-        both = mm_t(kept, jnp.concatenate([p, p], axis=0))
-        ch_o[pl.ds(rel, 1)] = jnp.where(lane_half == b, both, 0.0).astype(BF16)[None]
-        mine, here, there = child_copies(rel)
-
+    def children(*rels):
+        for rel in rels:
+            p = at(prj, rel)
+            kept = mm(p, at(fin, rel)).astype(BF16)
+            both = mm_t(kept, jnp.concatenate([p, p], axis=0))
+            ch_o[pl.ds(rel, 1)] = jnp.where(lane_half == b, both, 0.0).astype(BF16)[None]
+        for rel in rels:
+            send_child(*child_copies(rel))
+
+    def send_child(mine, here, there):
         @pl.when(mine)
         def _():
             here.start()
@@ -381,8 +390,8 @@
     def _():
         top_done(0, lower(0, 2), top)
 
-    for i in (4, 5):
-        loc_x[i].wait_recv()
+    for cp in loc_x["second"]:
+        cp.wait_recv()
 
     @pl.when(q == 0)
     def _():
@@ -392,9 +401,11 @@
     def _():
         bottom_done(0, upper(state(0, 1), 0))
 
+    for cp in cnt_x:
+        cp.wait_send()
     prj_x = []
     for i, (src, rel, dev) in enumerate(((uy, 3, to_up), (dy, 1, to_dn), (oy, 2, op))):
-        cp = rcopy(proj_h.at[src], prj.at[rel], prj_ss.at[i], prj_rs.at[i], dev)
+        cp = rcopy(proj_h.at[src], prj.at[rel], cnt_ss.at[i], prj_rs.at[i], dev)
         cp.start()
         prj_x.append(cp)
     combine(0, 1, lower(0, 0), upper(state(0, 2), 1))
@@ -403,16 +414,23 @@
     combine(1, 2, lower(1, 1), upper(st[1, 3], 2))
     low = lower(1, 2)
     high = upper(st[1, 1], 0)
+    mo[3] = lower(2, 2)
+    for ex in (link_x, loc_x):
+        for cp in [ex[2], ex[3]] + ex["second"]:
+            cp.wait_send()
     down_copy(1).wait_recv()
     combine(1, 3, low, upper(r_s[1], 3))
+    mo[2] = lower(2, 3)
+    for v in range(2):
+        up_copy(v).wait_send()
+    up_copy(2).start()
+    up_copy(3).start()
     up_copy(1).wait_recv()
     combine(1, 0, halo_low(r_m[1]), high)
+    for v in range(2):
+        down_copy(v).wait_send()
     down_copy(2).start()
     down_copy(3).start()
-    mo[2] = lower(2, 3)
-    up_copy(2).start()
-    mo[3] = lower(2, 2)
-    up_copy(3).start()
     combine(2, 1, lower(2, 0), upper(st[2, 2], 1))
     combine(2, 2, lower(2, 1), upper(st[2, 3], 2))
     for cp in edge_x:
@@ -424,24 +442,39 @@
     edge_inside = (rows < edge_cnt[0:1, 0:1]) & (cols < edge_cnt[0:1, 0:1])
     edge_sum[1] = r_s[0].astype(F32) - jnp.where(edge_inside, mo[2].astype(F32), 0.0)
     high = upper(st[2, 1], 0)
-    down_copy(2).wait_recv()
-    combine(2, 3, mo[3], upper(r_s[2], 3))
-    up_copy(2).wait_recv()
-    combine(2, 0, halo_low(r_m[2]), high)
     t = SWEEPS - 1
-    far_pos = 2 - q
-    near_pos = 1 + q
-    combine(t, far_pos, lower(t, far_pos - 1), upper(state(t, far_pos + 1), far_pos))
-    fin_x[0].start()
-    fin_x[1].start()
-    combine(t, near_pos, lower(t, near_pos - 1), upper(state(t, near_pos + 1), near_pos))
+
+    def interior(j):
+        combine(t, j, lower(t, j - 1), upper(st[t, j + 1], j))
+
+    def new_top():
+        down_copy(2).wait_recv()
+        combine(2, 3, mo[3], upper(r_s[2], 3))
+
+    def new_bottom():
+        up_copy(2).wait_recv()
+        combine(2, 0, halo_low(r_m[2]), high)
+
+    def far_back():
+        for cp in fin_x["first"]:
+            cp.start()
 
     @pl.when(q == 0)
     def _():
+        new_top()
+        interior(2)
+        far_back()
+        new_bottom()
+        interior(1)
         fin_x[2].start()
 
     @pl.when(q == 1)
     def _():
+        new_bottom()
+        interior(1)
+        far_back()
+        new_top()
+        interior(2)
         fin_x[3].start()
 
     low = lower(t, 2)
@@ -449,8 +482,7 @@
     own_prj.wait()
     for cp in prj_x:
         cp.wait_recv()
-    child(origin(1))
-    child(origin(2))
+    children(origin(1), origin(2))
     down_copy(t).wait_recv()
     above = edge_sum[1] - mm(edge_m[1], mm(r_s[t], edge_t[1]).astype(BF16))
     combine(t, 3, low, upper(above.astype(BF16), 3))
@@ -458,7 +490,7 @@
     @pl.when(q == 0)
     def _():
         last_lo[0].start()
-        child(3)
+        children(3)
         last_hi[0].start()
 
     up_copy(t).wait_recv()
@@ -469,13 +501,12 @@
     @pl.when(q == 1)
     def _():
         last_lo[1].start()
-        child(1)
+        children(1)
         last_hi[1].start()
 
-    child(0)
+    children(0)
     own_out.start()
-    relay(fin_x, 0)
-    relay(fin_x, 1)
+    relay(fin_x)
     far_cp.wait()
     for c in range(4):
         pltpu.make_async_copy(ch_o.at[0], ch_i.at[c], ch_rs.at[c]).wait()
@@ -485,8 +516,8 @@
     par_cp = pltpu.make_async_copy(far_v, par_ref.at[0], far_sem)
     par_cp.start()
 
-    for i in (4, 5):
-        fin_x[i].wait_recv()
+    for cp in fin_x["second"]:
+        cp.wait_recv()
     outer = (y == 0) | (y == GROUP - 1)
 
     @pl.when(outer)
@@ -502,9 +533,8 @@
 
     own_out.wait()
     par_cp.wait()
-    for ex, left in ((link_x, range(6)), (loc_x, range(6)), (fin_x, (0, 1, 4, 5))):
-        for i in left:
-            ex[i].wait_send()
+    for cp in fin_x["second"]:
+        cp.wait_send()
     for v in range(2):
 
         @pl.when(q == v)
@@ -513,11 +543,11 @@
             last_lo[v].wait_send()
             last_hi[v].wait_send()
 
-    for cp in cnt_x + prj_x:
+    for cp in prj_x:
         cp.wait_send()
     for cp in edge_x:
         cp.wait_send()
-    for t in range(SWEEPS):
+    for t in range(2, SWEEPS):
         down_copy(t).wait_send()
         up_copy(t).wait_send()
     for rel in range(GROUP):
@@ -595,17 +625,14 @@
             dma((4, 3)),
             dma,
             dma((3,)),
-            dma((3, 6)),
-            dma((3, 6)),
+            dma((2, 2 + 2 * PIECES)),
+            dma((3, 2 + 4 * PIECES)),
             dma((3,)),
             dma((3,)),
             dma((3,)),
-            dma((3,)),
-            dma((SWEEPS, 2)),
+            dma((2, 2)),
             dma((SWEEPS, 2)),
             dma((GROUP,)),
-            dma((GROUP,)),
-            dma((2,)),
             dma((2, 2)),
             dma((4,)),
             dma((4,)),

time: 50.5 us -> 50.3 us (level)
  no operation moved by 1% of the time
where the time goes in v5:
time: 50.3 us; the launch traced here: 50.1 us
  Pallas kernels  48.8 us (97%)
  between operations  1.29 us (3%)
    pallas_call x1, Pallas kernels, local(): pl.pallas_call(functools.partial(kernel, n_wide), name='skeleton', out_sh...  48 us

profile of v5, /device:TPU:6, one launch (start us, length us, event | category | flops | bytes accessed | tf_op | source)
XLA Modules:
  0.0 50.1 jit_solution(7150544314140309709)
XLA Ops:
  1.3 48.0 %skeleton.1 = (bf16[4,256,256]{2,1,0:T(8,128)(2,1)S(1)}, bf16[1,256,256]{2,1,0:T(8,128)(2,1)S(1)}) custom-call(s32[4]{0:T(128)} %pc_h.1, s32[1]{0:T(128)S(6)} %copy.10.bc_ref, bf16[4,256,256]{2,1,0:T(8,128)(2,1)} %self_h.1, bf16[4,256,512]{2,1,0:T(8,128)(2,1)} %cross_h.1, bf16[4,512,512]{2,1,0:T(8,128)(2,1)} %inv_h.1, bf16[4,256,256]{2,1,0:T(8,128)(2,1)} %link_h.1, ...), custom_call_target="tpu_custom_call" | custom-call | tf_op jit(solution)/shard_map/skeleton/pallas_call | solution.py:592
  49.3 0.8 %settle.1 = (bf16[4,256,256]{2,1,0:T(8,128)(2,1)}, bf16[1,256,256]{2,1,0:T(8,128)(2,1)}) custom-call(bf16[4,256,256]{2,1,0:T(8,128)(2,1)S(1)} %get-tuple-element.4.out_v, bf16[1,256,256]{2,1,0:T(8,128)(2,1)S(1)} %get-tuple-element.5.par_v), custom_call_target="tpu_custom_call" | custom-call | tf_op jit(solution)/shard_map/settle/pallas_call | solution.py:658

commit v6 on v5

--- a/solution.py
+++ b/solution.py
@@ -441,11 +441,18 @@
     edge_sum[0] = edge_loc[...].astype(F32) - edge_high
     edge_inside = (rows < edge_cnt[0:1, 0:1]) & (cols < edge_cnt[0:1, 0:1])
     edge_sum[1] = r_s[0].astype(F32) - jnp.where(edge_inside, mo[2].astype(F32), 0.0)
-    high = upper(st[2, 1], 0)
+    high_2 = upper(st[2, 1], 0)
     t = SWEEPS - 1
+    low = lower(t, 2)
+    high = upper(st[t, 1], 0)
+    inner_low = lower(t, 1)
+    inner_high = upper(st[t, 2], 1)
 
     def interior(j):
-        combine(t, j, lower(t, j - 1), upper(st[t, j + 1], j))
+        if j == 1:
+            combine(t, 1, lower(t, 0), inner_high)
+        else:
+            combine(t, 2, inner_low, upper(st[t, 3], 2))
 
     def new_top():
         down_copy(2).wait_recv()
@@ -453,7 +460,7 @@
 
     def new_bottom():
         up_copy(2).wait_recv()
-        combine(2, 0, halo_low(r_m[2]), high)
+        combine(2, 0, halo_low(r_m[2]), high_2)
 
     def far_back():
         for cp in fin_x["first"]:
@@ -477,34 +484,32 @@
         interior(2)
         fin_x[3].start()
 
-    low = lower(t, 2)
-    high = upper(st[t, 1], 0)
     own_prj.wait()
     for cp in prj_x:
         cp.wait_recv()
-    children(origin(1), origin(2))
-    down_copy(t).wait_recv()
-    above = edge_sum[1] - mm(edge_m[1], mm(r_s[t], edge_t[1]).astype(BF16))
-    combine(t, 3, low, upper(above.astype(BF16), 3))
-
-    @pl.when(q == 0)
-    def _():
-        last_lo[0].start()
-        children(3)
-        last_hi[0].start()
-
-    up_copy(t).wait_recv()
-    below = (edge_sum[0] - r_m[t].astype(F32)).astype(BF16)
-    below_low = mm(edge_t[0], mm(below, edge_m[0]).astype(BF16)).astype(BF16)
-    combine(t, 0, halo_low(below_low), high)
-
-    @pl.when(q == 1)
-    def _():
-        last_lo[1].start()
-        children(1)
-        last_hi[1].start()
-
-    children(0)
+
+    def last_top():
+        down_copy(t).wait_recv()
+        above = edge_sum[1] - mm(edge_m[1], mm(r_s[t], edge_t[1]).astype(BF16))
+        combine(t, 3, low, upper(above.astype(BF16), 3))
+
+    def last_bottom():
+        up_copy(t).wait_recv()
+        below = (edge_sum[0] - r_m[t].astype(F32)).astype(BF16)
+        below_low = mm(edge_t[0], mm(below, edge_m[0]).astype(BF16)).astype(BF16)
+        combine(t, 0, halo_low(below_low), high)
+
+    for v, steps in enumerate(((last_top, last_bottom), (last_bottom, last_top))):
+
+        @pl.when(q == v)
+        def _():
+            steps[0]()
+            last_lo[v].start()
+            children(1, 2, 3)
+            last_hi[v].start()
+            steps[1]()
+            children(0)
+
     own_out.start()
     relay(fin_x)
     far_cp.wait()

time: 50.3 us -> 49 us (0.974)
  Pallas kernels: 48.8 us -> 47.6 us
    pallas_call x1, Pallas kernels: 48 us -> 46.8 us  [local(): pl.pallas_call(functools.partial(kernel, n_wide), name='skeleton', out_sh...]
where the time goes in v6:
time: 49 us; the launch traced here: 48.9 us
  Pallas kernels  47.6 us (97%)
  between operations  1.29 us (3%)
    pallas_call x1, Pallas kernels, local(): pl.pallas_call(functools.partial(kernel, n_wide), name='skeleton', out_sh...  46.8 us

profile of v6, /device:TPU:6, one launch (start us, length us, event | category | flops | bytes accessed | tf_op | source)
XLA Modules:
  0.0 48.9 jit_solution(11002819134604058982)
XLA Ops:
  1.3 46.8 %skeleton.1 = (bf16[4,256,256]{2,1,0:T(8,128)(2,1)S(1)}, bf16[1,256,256]{2,1,0:T(8,128)(2,1)S(1)}) custom-call(s32[4]{0:T(128)} %pc_h.1, s32[1]{0:T(128)S(6)} %copy.10.bc_ref, bf16[4,256,256]{2,1,0:T(8,128)(2,1)} %self_h.1, bf16[4,256,512]{2,1,0:T(8,128)(2,1)} %cross_h.1, bf16[4,512,512]{2,1,0:T(8,128)(2,1)} %inv_h.1, bf16[4,256,256]{2,1,0:T(8,128)(2,1)} %link_h.1, ...), custom_call_target="tpu_custom_call" | custom-call | tf_op jit(solution)/shard_map/skeleton/pallas_call | solution.py:597
  48.1 0.8 %settle.1 = (bf16[4,256,256]{2,1,0:T(8,128)(2,1)}, bf16[1,256,256]{2,1,0:T(8,128)(2,1)}) custom-call(bf16[4,256,256]{2,1,0:T(8,128)(2,1)S(1)} %get-tuple-element.4.out_v, bf16[1,256,256]{2,1,0:T(8,128)(2,1)S(1)} %get-tuple-element.5.par_v), custom_call_target="tpu_custom_call" | custom-call | tf_op jit(solution)/shard_map/settle/pallas_call | solution.py:663

commit v7 on v6

--- a/solution.py
+++ b/solution.py
@@ -564,10 +564,9 @@
 
 
 def settle(out_v, par_v, out_h, par_h, sem):
-    copies = (
-        pltpu.make_async_copy(out_v, out_h, sem.at[0]),
-        pltpu.make_async_copy(par_v, par_h, sem.at[1]),
-    )
+    slots = out_v.shape[0]
+    copies = [pltpu.make_async_copy(out_v.at[i], out_h.at[i], sem.at[i]) for i in range(slots)]
+    copies.append(pltpu.make_async_copy(par_v, par_h, sem.at[slots]))
     for cp in copies:
         cp.start()
     for cp in copies:
@@ -666,7 +665,7 @@
         out_shape=shapes,
         in_specs=[hbm] * 2,
         out_specs=(hbm, hbm),
-        scratch_shapes=[dma((2,))],
+        scratch_shapes=[dma((slots + 1,))],
     )(*(pltpu.with_memory_space_constraint(x, pltpu.VMEM) for x in results))
 
 

time: 49 us -> 49.1 us (level)
  no operation moved by 1% of the time
where the time goes in v7:
time: 49.1 us; the launch traced here: 48.9 us
  Pallas kernels  47.7 us (97%)
  between operations  1.29 us (3%)
    pallas_call x1, Pallas kernels, local(): pl.pallas_call(functools.partial(kernel, n_wide), name='skeleton', out_sh...  46.8 us

profile of v7, /device:TPU:6, one launch (start us, length us, event | category | flops | bytes accessed | tf_op | source)
XLA Modules:
  0.0 48.9 jit_solution(2102992956901882685)
XLA Ops:
  1.3 46.8 %skeleton.1 = (bf16[4,256,256]{2,1,0:T(8,128)(2,1)S(1)}, bf16[1,256,256]{2,1,0:T(8,128)(2,1)S(1)}) custom-call(s32[4]{0:T(128)} %pc_h.1, s32[1]{0:T(128)S(6)} %copy.10.bc_ref, bf16[4,256,256]{2,1,0:T(8,128)(2,1)} %self_h.1, bf16[4,256,512]{2,1,0:T(8,128)(2,1)} %cross_h.1, bf16[4,512,512]{2,1,0:T(8,128)(2,1)} %inv_h.1, bf16[4,256,256]{2,1,0:T(8,128)(2,1)} %link_h.1, ...), custom_call_target="tpu_custom_call" | custom-call | tf_op jit(solution)/shard_map/skeleton/pallas_call | solution.py:596
  48.1 0.9 %settle.1 = (bf16[4,256,256]{2,1,0:T(8,128)(2,1)}, bf16[1,256,256]{2,1,0:T(8,128)(2,1)}) custom-call(bf16[4,256,256]{2,1,0:T(8,128)(2,1)S(1)} %get-tuple-element.4.out_v, bf16[1,256,256]{2,1,0:T(8,128)(2,1)S(1)} %get-tuple-element.5.par_v), custom_call_target="tpu_custom_call" | custom-call | tf_op jit(solution)/shard_map/settle/pallas_call | solution.py:662
